TPU v7x, 128 devices: a whole 4x4x4 slice. The times are simulated.
128 devices in a mesh: dir: 32 (over y, x, core), region: 4 (over z).
Axes of the slice: x: 4, y: 4, z: 4, core: 2. Of those that a mesh axis runs over, the one named last changes fastest.
Arguments:
- currents: bfloat16 [4, 192, 128, 256], P('region', 'dir'), may hold values from -6 to 6
- radiate: bfloat16 [1536, 128], replicated, may hold values from -0.5 to 0.5
- receive: bfloat16 [128, 1536], replicated, may hold values from -0.15625 to 0.15625
- transfer_table: bfloat16 [316, 1536], replicated, may hold values from -0.875 to 0.875
- near_blocks: bfloat16 [4, 192, 27, 128, 128], P('region', 'dir'), may hold values from -0.109375 to 0.109375
- dir_offsets: int32 [33], replicated, may hold values from 0 to 1536, as said below
- trans_src: int32 [4, 192, 48], P('region'), may hold values from -1 to 383, as said below
- trans_tid: int32 [4, 192, 48], P('region'), may hold values from 0 to 315
- near_src: int32 [4, 192, 27], P('region', 'dir'), may hold values from -1 to 287, as said below
Outputs:
- scattered: bfloat16 [4, 192, 128, 256], P('region', 'dir')
Inputs may be any that keep to these rules, and one draw needn't show every extreme that they name: dir_offsets starts at 0, ends at 1536 and rises; every band holds 24 to 72 direction samples, and some band holds exactly 72. `trans_src`: in each box's list the non-empty slots come first and name distinct boxes; a list holds 24 to 48 of them, and some list is full. `near_src`: each box's list starts with the box itself, then names distinct other boxes, then empty slots; a list holds 13 to 27 non-empty slots, and some list is full.
All inputs are finite; a program needn't handle non-finite values.
Results may differ from a plain program's by a relative error of at most 0.005.
Values may be sent and summed in bfloat16 or wider, within the bound.
A program may use at most 192 MiB of HBM per device.

v0:
```python
import jax
import jax.numpy as jnp
from jax import lax
from jax.sharding import PartitionSpec as P


def padded(array, sides, width):
    for axis, dim in sides:
        devices, length = (lax.axis_size(axis), array.shape[dim])
        up = [(i, (i + 1) % devices) for i in range(devices - 1)]
        down = [(j, i) for i, j in up]
        last = lax.slice_in_dim(array, length - width, length, axis=dim)
        initial = lax.slice_in_dim(array, 0, width, axis=dim)
        before = lax.ppermute(last, axis, up)
        after = lax.ppermute(initial, axis, down)
        array = jnp.concatenate([before, array, after], axis=dim)
    return array


def band_weights(offsets, directions):
    dir_count = offsets.shape[0] - 1
    position = jnp.arange(directions, dtype=jnp.int32)
    starts = offsets[:-1]
    band_ends = offsets[1:]
    inside = (position[None, :] >= starts[:, None]) & (position[None, :] < band_ends[:, None])
    per_band = directions / (dir_count * (band_ends - starts).astype(jnp.float32))
    return jnp.sum(jnp.where(inside, per_band[:, None], jnp.zeros((), jnp.float32)), axis=0)


def shards(
    currents,
    radiate,
    receive,
    transfer_table,
    near_blocks,
    dir_offsets,
    trans_src,
    trans_tid,
    near_src,
):
    dir_count = lax.axis_size("dir")
    dir_index = lax.axis_index("dir")
    own_field = currents[0]
    box_count = own_field.shape[0]
    incidences = own_field.shape[2]
    directions = radiate.shape[0]
    classes = transfer_table.shape[0]
    zero_value = jnp.zeros((), jnp.bfloat16)
    weights = band_weights(dir_offsets, directions)
    recv_w = (receive.astype(jnp.float32) * weights[None, :]).astype(jnp.bfloat16)
    band_width = directions // dir_count
    coef_used = lax.dynamic_slice_in_dim(transfer_table, dir_index * band_width, band_width, 1)
    region_count = box_count * dir_count
    region_field = lax.all_gather(own_field, "dir", axis=0, tiled=True)
    outgoing = jnp.einsum(
        "kq,bqr->bkr", radiate, own_field, preferred_element_type=jnp.float32
    ).astype(jnp.bfloat16)
    outgoing = outgoing.reshape(box_count, dir_count, band_width, incidences)
    spectra = lax.all_to_all(outgoing, "dir", split_axis=1, concat_axis=0, tiled=True)
    spectra = spectra.reshape(region_count, band_width, incidences)
    extended = padded(spectra, (("region", 0),), region_count // 2)
    near_ext = padded(region_field, (("region", 0),), region_count // 4)
    ext_span = extended.shape[0]
    sources = trans_src[0]
    source_hot = (sources[:, :, None] == lax.iota(jnp.int32, ext_span)[None, None, :]).astype(
        jnp.bfloat16
    )
    class_hot = (trans_tid[0][:, :, None] == lax.iota(jnp.int32, classes)[None, None, :]).astype(
        jnp.bfloat16
    )
    pair_hot = jnp.einsum(
        "jls,jln->jsn", source_hot, class_hot, preferred_element_type=jnp.float32
    ).astype(jnp.bfloat16)
    matrix = jnp.einsum(
        "jsn,nt->tjs", pair_hot, coef_used, preferred_element_type=jnp.float32
    ).astype(jnp.bfloat16)
    translated = jnp.einsum(
        "tjs,str->jtr", matrix, extended, preferred_element_type=jnp.float32
    ).astype(jnp.bfloat16)
    translated = translated.reshape(dir_count, box_count, 1, band_width, incidences)
    returned = lax.all_to_all(translated, "dir", split_axis=0, concat_axis=2, tiled=True)
    returned = returned.reshape(box_count, dir_count * band_width, incidences)
    far_field = jnp.einsum("qc,bcr->bqr", recv_w, returned, preferred_element_type=jnp.float32)
    near_here = near_src[0]
    picked = jnp.take(near_ext, jnp.maximum(near_here, 0), axis=0)
    picked = jnp.where((near_here >= 0)[:, :, None, None], picked, zero_value)
    near_field = jnp.einsum(
        "bmpq,bmqr->bpr", near_blocks[0], picked, preferred_element_type=jnp.float32
    )
    return (far_field + near_field).astype(jnp.bfloat16)[None]


def solution(mesh):
    placed = (
        P("region", "dir", None, None),
        P(),
        P(),
        P(),
        P("region", "dir", None, None, None),
        P(),
        P("region", None, None),
        P("region", None, None),
        P("region", "dir", None),
    )
    return jax.shard_map(
        shards,
        mesh=mesh,
        in_specs=placed,
        out_specs=P("region", "dir", None, None),
        check_vma=False,
    )
```

profile of v0, /device:TPU:1, one launch (start us, length us, event | category | flops | bytes accessed | tf_op | source)
XLA Modules:
  0.0 334.0 jit_solution(2451714476054266654)
XLA Ops:
  7.3 4.7 %convert_bitcast_fusion.1 = bf16[6,1536,256]{1,2,0:T(8,128)(2,1)} fusion(bf16[1536,128]{1,0:T(8,128)(2,1)} %param.10, bf16[1,6,128,256]{3,2,1,0:T(8,128)(2,1)} %param.9), kind=kOutput, calls=%fused_computation.26 | convolution fusion | flops 606339072 | bytes 5505024 | tf_op jit(solution)/shard_map/kq,bqr->bkr/dot_general | solution.py:55
  11.9 6.7 %copy.52 = bf16[6,1536,256]{2,1,0:T(8,128)(2,1)} copy(bf16[6,1536,256]{1,2,0:T(8,128)(2,1)} %convert_bitcast_fusion.1) | data formatting | bytes 9437184 | tf_op jit(solution)/shard_map/convert_element_type | solution.py:57
  18.6 2.9 copy.53
  21.5 83.3 %all_to_all.30 = bf16[6,32,48,256]{3,2,0,1:T(8,128)(2,1)S(1)} all-to-all(bf16[6,32,48,256]{3,2,0,1:T(8,128)(2,1)S(1)} %copy.53), channel_id=1, replica_groups=mesh['dir'=32,'region'=4] {'dir'}, dimensions={1} | all-to-all | bytes 9437184 | tf_op jit(solution)/shard_map/all_to_all | solution.py:59
  108.1 2.2 copy.54
  110.4 5.5 %collective-permute-start = (bf16[96,48,256]{2,0,1:T(8,128)(2,1)}, bf16[96,48,256]{2,0,1:T(8,128)(2,1)}, u32[]{:S(2)}, u32[]{:S(2)}) collective-permute-start(bf16[96,48,256]{2,0,1:T(8,128)(2,1)} %copy.54), channel_id=1, source_target_pairs={{0,1},{1,2},{2,3},{4,5},{5,6},{6,7},{8,9},{9,10},{10,11},{12,13},{... | collective-permute-start | bytes 7077896 | tf_op jit(solution)/shard_map/ppermute | solution.py:14
  117.6 27.3 %fusion.20 = bf16[48,192,384]{2,0,1:T(8,128)(2,1)} fusion(s32[192,48]{1,0:T(8,128)S(1)} %copy.59, s32[192,48]{1,0:T(8,128)S(1)} %copy.58, bf16[316,48,1]{1,0,2:T(8,128)(2,1)} %fusion.58), kind=kOutput, calls=%fused_computation.21 | convolution fusion | flops 4506513408 | bytes 7181952 | tf_op jit(solution)/shard_map/jsn,nt->tjs/dot_general | solution.py:74
  144.9 6.2 %copy.56 = bf16[192,48,256]{2,0,1:T(8,128)(2,1)} copy(bf16[192,48,256]{2,1,0:T(8,128)(2,1)} %bitcast.65) | data formatting | bytes 9437184 | tf_op jit(solution)/shard_map/reshape | solution.py:60
  151.1 10.2 %collective-permute-done.1 = bf16[96,48,256]{2,0,1:T(8,128)(2,1)} collective-permute-done((bf16[96,48,256]{2,0,1:T(8,128)(2,1)S(1)}, bf16[96,48,256]{2,0,1:T(8,128)(2,1)}, u32[]{:S(2)}, u32[]{:S(2)}) %collective-permute-start.1) | collective-permute-done | bytes 2359328 | tf_op jit(solution)/shard_map/ppermute | solution.py:15
  161.3 3.3 collective-permute-done
  164.6 12.7 %convert_bitcast_fusion = bf16[192,48,256]{2,0,1:T(8,128)(2,1)} fusion(bf16[96,48,256]{2,0,1:T(8,128)(2,1)} %collective-permute-done.1, bf16[192,48,256]{2,0,1:T(8,128)(2,1)} %copy.56, bf16[96,48,256]{2,0,1:T(8,128)(2,1)} %collective-permute-done, bf16[48,192,384]{2,0,1:T(8,128)(2,1)} %fusion.20), kind=kOutput, calls=%fused_computation.25 | convolution fusion | flops 1842610176 | bytes 21233664 | tf_op jit(solution)/shard_map/tjs,str->jtr/dot_general | solution.py:77
  177.3 7.2 %copy.61 = bf16[192,48,256]{2,1,0:T(8,128)(2,1)} copy(bf16[192,48,256]{2,0,1:T(8,128)(2,1)} %convert_bitcast_fusion) | data formatting | bytes 9437184 | tf_op jit(solution)/shard_map/convert_element_type | solution.py:79
  184.4 7.3 %all-to-all-start.1 = ((bf16[32,6,1,48,256]{4,3,1,2,0:T(8,128)(2,1)}), bf16[32,6,1,48,256]{4,3,1,2,0:T(8,128)(2,1)}, u32[]{:S(2)}, u32[]{:S(2)}) async-start(bf16[32,6,1,48,256]{4,3,1,2,0:T(8,128)(2,1)} %bitcast.71), calls=%async_computation.1 | async-start | bytes 9437184 | tf_op jit(solution)/shard_map/all_to_all | solution.py:81
  191.7 6.3 %slice_bitcast_fusion.1 = (bf16[48,128,256]{2,1,0:T(8,128)(2,1)}, bf16[48,128,256]{2,1,0:T(8,128)(2,1)}) fusion(bf16[1,192,128,256]{3,2,0,1:T(8,128)(2,1)} %all-gather.3.cloned.1.call-done), kind=kLoop, calls=%fused_computation.28 | loop fusion | bytes 12582912 | tf_op jit(solution)/shard_map/slice | solution.py:12
  199.4 6.4 %collective-permute-start.2 = (bf16[48,128,256]{2,1,0:T(8,128)(2,1)}, bf16[48,128,256]{2,1,0:T(8,128)(2,1)}, u32[]{:S(2)}, u32[]{:S(2)}) collective-permute-start(bf16[48,128,256]{2,1,0:T(8,128)(2,1)} %get-tuple-element.5), channel_id=1, source_target_pairs={{0,1},{1,2},{2,3},{4,5},{5,6},{6,7},{8,9},{9,10},{10,11},{12,13},{... | collective-permute-start | bytes 9437192 | tf_op jit(solution)/shard_map/ppermute | solution.py:14
  206.2 41.5 %all-to-all-done.1 = bf16[32,6,1,48,256]{4,3,1,2,0:T(8,128)(2,1)} async-done(((bf16[32,6,1,48,256]{4,3,1,2,0:T(8,128)(2,1)}), bf16[32,6,1,48,256]{4,3,1,2,0:T(8,128)(2,1)}, u32[]{:S(2)}, u32[]{:S(2)}) %all-to-all-start.1) | async-done | bytes 4718624 | tf_op jit(solution)/shard_map/all_to_all | solution.py:81
  247.8 4.9 %copy.63 = bf16[32,6,1,48,256]{4,3,0,1,2:T(8,128)(2,1)} copy(bf16[32,6,1,48,256]{4,3,1,2,0:T(8,128)(2,1)} %all-to-all-done.1) | data formatting | bytes 9437184 | tf_op jit(solution)/shard_map/all_to_all | solution.py:81
  252.7 18.0 %collective-permute-done.3 = bf16[48,128,256]{2,1,0:T(8,128)(2,1)} collective-permute-done((bf16[48,128,256]{2,1,0:T(8,128)(2,1)}, bf16[48,128,256]{2,1,0:T(8,128)(2,1)}, u32[]{:S(2)}, u32[]{:S(2)}) %collective-permute-start.3) | collective-permute-done | bytes 3145760 | tf_op jit(solution)/shard_map/ppermute | solution.py:15
  271.6 15.2 %pad_maximum_fusion = bf16[288,128,256]{2,1,0:T(8,128)(2,1)} fusion(bf16[48,128,256]{2,1,0:T(8,128)(2,1)} %collective-permute-done.3, bf16[192,128,256]{2,1,0:T(8,128)(2,1)} %bitcast.70, bf16[48,128,256]{2,1,0:T(8,128)(2,1)} %collective-permute-done.2), kind=kLoop, calls=%fused_computation.4 | loop fusion | flops 18874368 | bytes 37748736 | tf_op jit(solution)/shard_map/concatenate | solution.py:16
  286.7 14.0 %gather_fusion = bf16[162,128,256]{2,1,0:T(8,128)(2,1)} fusion(bf16[288,128,256]{2,1,0:T(8,128)(2,1)} %pad_maximum_fusion, s32[1024]{0:T(1024)S(1)} %pad_clamp_fusion), kind=kCustom, calls=%fused_computation | custom fusion | bytes 21234312 | tf_op jit(solution)/shard_map/jit(_take)/gather | solution.py:85
  300.7 13.9 %copy.66 = bf16[6,27,128,256]{2,3,1,0:T(8,128)(2,1)} copy(bf16[6,27,128,256]{3,2,1,0:T(8,128)(2,1)} %bitcast.66) | data formatting | bytes 21233664 | tf_op jit(solution)/shard_map/jit(_take)/gather | solution.py:85
  314.7 7.4 %fusion.30 = f32[6,256,128]{2,1,0:T(8,128)S(1)} fusion(bf16[1,6,27,128,128]{4,3,2,1,0:T(8,128)(2,1)} %param.13, bf16[6,27,128,256]{2,3,1,0:T(8,128)(2,1)} %copy.66, pred[6,27]{1,0:T(8,128)(4,1)S(1)} %get-tuple-element.13, pred[6,27]{1,0:T(8,128)(4,1)S(1)} %get-tuple-element.14), kind=kOutput, calls=%fused_computation.30 | convolution fusion | flops 1369571328 | bytes 16712004 | tf_op jit(solution)/shard_map/bmpq,bmqr->bpr/dot_general | solution.py:87
  322.1 3.2 fusion.36
  325.3 1.9 copy.67
  (36 shorter events, 8.4 us)
Async XLA Ops:
  6.5 110.3 %copy-start = (bf16[316,1536]{1,0:T(8,128)(2,1)S(1)}, bf16[316,1536]{1,0:T(8,128)(2,1)}, u32[]{:S(2)}) copy-start(bf16[316,1536]{1,0:T(8,128)(2,1)} %param.12) | copy-start | bytes 2912260
  6.5 185.2 %all-gather.3.cloned.1.call-start = ((), (), s32[]{:S(2)}) async-start(), calls=%async_computation.2 | async-start | bytes 12976128 | tf_op jit(solution)/shard_map/all_gather | solution.py:54
  104.8 2.1 copy-start.2
  105.1 10.8 %copy-start.3 = (s32[1,192,48]{1,2,0:T(8,128)S(1)}, s32[1,192,48]{1,2,0:T(8,128)}, u32[]{:S(2)}) copy-start(s32[1,192,48]{1,2,0:T(8,128)} %param.16) | copy-start | bytes 110596
  106.9 54.4 %collective-permute-start.1 = (bf16[96,48,256]{2,0,1:T(8,128)(2,1)S(1)}, bf16[96,48,256]{2,0,1:T(8,128)(2,1)}, u32[]{:S(2)}, u32[]{:S(2)}) collective-permute-start(bf16[96,48,256]{2,0,1:T(8,128)(2,1)S(1)} %copy.55), channel_id=1, source_target_pairs={{1,0},{2,1},{3,2},{5,4},{6,5},{7,6},{9,8},{10,9},{11,10},{13,12},{... | collective-permute-start | bytes 7077896 | tf_op jit(solution)/shard_map/ppermute | solution.py:15
  110.4 54.2 %collective-permute-start = (bf16[96,48,256]{2,0,1:T(8,128)(2,1)}, bf16[96,48,256]{2,0,1:T(8,128)(2,1)}, u32[]{:S(2)}, u32[]{:S(2)}) collective-permute-start(bf16[96,48,256]{2,0,1:T(8,128)(2,1)} %copy.54), channel_id=1, source_target_pairs={{0,1},{1,2},{2,3},{4,5},{5,6},{6,7},{8,9},{9,10},{10,11},{12,13},{... | collective-permute-start | bytes 7077896 | tf_op jit(solution)/shard_map/ppermute | solution.py:14
  184.4 63.3 %all-to-all-start.1 = ((bf16[32,6,1,48,256]{4,3,1,2,0:T(8,128)(2,1)}), bf16[32,6,1,48,256]{4,3,1,2,0:T(8,128)(2,1)}, u32[]{:S(2)}, u32[]{:S(2)}) async-start(bf16[32,6,1,48,256]{4,3,1,2,0:T(8,128)(2,1)} %bitcast.71), calls=%async_computation.1 | async-start | bytes 9437184 | tf_op jit(solution)/shard_map/all_to_all | solution.py:81
  191.7 14.1 %copy-start.4 = (s32[1,6,27]{2,0,1:T(1,128)S(1)}, s32[1,6,27]{2,0,1:T(1,128)}, u32[]{:S(2)}) copy-start(s32[1,6,27]{2,0,1:T(1,128)} %param.17) | copy-start | bytes 1948
  191.7 14.2 %copy-start.5 = (s32[33]{0:T(128)S(1)}, s32[33]{0:T(128)}, u32[]{:S(2)}) copy-start(s32[33]{0:T(128)} %param.14) | copy-start | bytes 400
  198.1 72.6 %collective-permute-start.3 = (bf16[48,128,256]{2,1,0:T(8,128)(2,1)}, bf16[48,128,256]{2,1,0:T(8,128)(2,1)}, u32[]{:S(2)}, u32[]{:S(2)}) collective-permute-start(bf16[48,128,256]{2,1,0:T(8,128)(2,1)} %get-tuple-element.6), channel_id=1, source_target_pairs={{1,0},{2,1},{3,2},{5,4},{6,5},{7,6},{9,8},{10,9},{11,10},{13,12},{... | collective-permute-start | bytes 9437192 | tf_op jit(solution)/shard_map/ppermute | solution.py:15
  199.4 72.2 %collective-permute-start.2 = (bf16[48,128,256]{2,1,0:T(8,128)(2,1)}, bf16[48,128,256]{2,1,0:T(8,128)(2,1)}, u32[]{:S(2)}, u32[]{:S(2)}) collective-permute-start(bf16[48,128,256]{2,1,0:T(8,128)(2,1)} %get-tuple-element.5), channel_id=1, source_target_pairs={{0,1},{1,2},{2,3},{4,5},{5,6},{6,7},{8,9},{9,10},{10,11},{12,13},{... | collective-permute-start | bytes 9437192 | tf_op jit(solution)/shard_map/ppermute | solution.py:14
  300.7 21.3 %slice-start = ((s8[4718592]{0:T(1024)(128)(4,1)}), s8[524288]{0:T(1024)(128)(4,1)S(1)}, s32[]{:S(2)}) async-start(s8[4718592]{0:T(1024)(128)(4,1)} %bitcast.67), calls=%async_computation.3 | async-start | bytes 1048576
  314.7 7.4 %slice-start.1 = ((s8[4718592]{0:T(1024)(128)(4,1)}), s8[4194304]{0:T(1024)(128)(4,1)S(1)}, s32[]{:S(2)}) async-start(s8[4718592]{0:T(1024)(128)(4,1)} %bitcast.67), calls=%async_computation.4 | async-start | bytes 8388608
  314.7 12.5 %copy-start.1 = (bf16[316,1536]{1,0:T(8,128)(2,1)S(1)}, bf16[316,1536]{1,0:T(8,128)(2,1)}, u32[]{:S(2)}) copy-start(bf16[316,1536]{1,0:T(8,128)(2,1)} %param.12) | copy-start | bytes 2912260
Sparse Core Ops, SparseCore 0:
  9.6 104.3 all-gather.2
where the time goes:
time: 339 us; the launch traced here: 334 us
  blocking collectives  83.3 us (25%)
  waiting for transfers between devices  74.6 us (22%)
  local copies, waits for them, and re-layouts  70.2 us (21%)
  matrix products  55.2 us (16%)
  starting transfers between devices  21.7 us (6%)
  other arithmetic  15.4 us (5%)
  between operations  13.6 us (4%)
    all_to_all x1, blocking collectives, shards(): lax.all_to_all(outgoing, 'dir', split_axis=1, concat_axis=0, tiled=True)  83.3 us
    all_to_all x1, waiting for transfers between devices, shards(): lax.all_to_all(translated, 'dir', split_axis=0, concat_axis=2, tiled=True)  41.5 us
    ppermute x2, waiting for transfers between devices, padded(): after = lax.ppermute(initial, axis, down)  28.1 us
    gather x2, local copies, waits for them, and re-layouts, shards(): picked = jnp.take(near_ext, jnp.maximum(near_here, 0), axis=0)  27.9 us
    dot_general x1, matrix products, shards(): jnp.einsum('jsn,nt->tjs', pair_hot, coef_used, preferred_element_type=jnp...  27.3 us
    concatenate x1, other arithmetic, padded(): array = jnp.concatenate([before, array, after], axis=dim)  15.2 us
    dot_general x1, matrix products, shards(): jnp.einsum('tjs,str->jtr', matrix, extended, preferred_element_type=jnp.f...  12.7 us
    ppermute x2, starting transfers between devices, padded(): before = lax.ppermute(last, axis, up)  11.9 us
  transfers between devices with their start and end apart: 6, of which 5 were waited for; matrix products, arithmetic and copies ran while one was open for 25% of the time, Pallas kernels for 0%

commit v1 on v0

v1 whole, which is shorter than its diff:
```python
import jax
import jax.numpy as jnp
from jax import lax
from jax.experimental import pallas as pl
from jax.experimental.pallas import tpu as pltpu
from jax.sharding import PartitionSpec as P

MESH = pl.DeviceIdType.MESH
BF = jnp.bfloat16
F32 = jnp.float32
TB = 96
NCH = 6
TCH = TB // NCH


def m4(v):
    return lax.rem(v + 8, 4)


def body(
    cur_in, rad_in, rcv_in, nb_in, nsl_in, tt_t, src, tid, offs, out,
    cur, nb, mat, pat, tx, rx, relay, ps, pr, acc, buf, rad, rcv, rw, fin, nsv, ns_own, ns_par,
    lsem, psend, precv, asend, arecv, zsend, zrecv, rsend, rrecv, ssend, srecv,
):
    d = lax.axis_index("dir")
    z = lax.axis_index("region")
    c = lax.rem(d, 2)
    chip = lax.div(d, 2)
    x = lax.rem(chip, 4)
    y = lax.div(chip, 4)
    pa = x + c * (y - x)
    pb = y + c * (x - y)
    oc = 1 - c

    def dev(a, b, zz=None):
        xx = a + c * (b - a)
        yy = b + c * (a - b)
        return ((yy * 4 + xx) * 2 + c, z if zz is None else zz)

    partner = (d + 1 - 2 * c, z)
    a_up, a_dn = dev(m4(pa + 1), pb), dev(m4(pa - 1), pb)
    b_up, b_dn = dev(pa, m4(pb + 1)), dev(pa, m4(pb - 1))
    b_far = dev(pa, m4(pb + 2))
    z_up, z_dn = dev(pa, pb, m4(z + 1)), dev(pa, pb, m4(z - 1))

    barrier = pltpu.get_barrier_semaphore()
    for peer in (partner, a_up, a_dn, b_up, b_dn, b_far, z_up, z_dn):
        pl.semaphore_signal(barrier, inc=1, device_id=peer, device_id_type=MESH)
    pl.semaphore_wait(barrier, 8)

    pending = []

    def remote(src_ref, dst_ref, send, recv, to):
        return pltpu.make_async_remote_copy(
            src_ref=src_ref, dst_ref=dst_ref, send_sem=send, recv_sem=recv,
            device_id=to, device_id_type=MESH,
        )

    def go(copy):
        copy.start()
        pending.append(copy)
        return copy

    def base(oa, ob):
        return pl.multiple_of((m4(pa - oa) * 4 + m4(pb - ob)) * 16, 16)

    own0 = base(0, 0)
    give = remote(
        cur_in.at[:, :, pl.ds(pl.multiple_of(oc * 128, 128), 128)],
        cur.at[pl.ds((pb * 4 + pa) * 16 + c * 6, 6)],
        psend.at[0], precv.at[0], partner,
    )
    go(give)
    keep = pltpu.make_async_copy(
        cur_in.at[:, :, pl.ds(pl.multiple_of(c * 128, 128), 128)],
        cur.at[pl.ds(own0 + c * 6, 6)], lsem.at[0],
    )
    keep.start()
    band = pb * 4 + pa
    load_rad = pltpu.make_async_copy(
        rad_in.at[pl.ds(pl.multiple_of(band * TB, 16), TB)], rad, lsem.at[1]
    )
    load_rad.start()
    load_rcv = pltpu.make_async_copy(
        rcv_in.at[:, pl.ds(pl.multiple_of(pb * 384, 128), 384)], rcv, lsem.at[2]
    )
    load_rcv.start()
    load_ns = pltpu.make_async_copy(nsl_in.at[pl.ds(0, 8)], ns_own, lsem.at[3])
    load_ns.start()
    give_ns = remote(nsl_in.at[pl.ds(8, 8)], nsv, psend.at[1], precv.at[1], partner)
    go(give_ns)

    def arrived(ref, sem):
        remote(ref, ref, psend.at[0], sem, partner).wait_recv()

    count = [0]

    def send_main(oa, ob, lo, n, to, ra, rb, piece):
        part = cur.at[pl.ds(base(oa, ob) + lo, n)]
        go(remote(part, part, asend.at[count[0]], arecv.at[(ra * 4 + rb) * 2 + piece], to))
        count[0] += 1

    def got_main(oa, ob, lo, n, piece):
        arrived(cur.at[pl.ds(base(oa, ob) + lo, n)], arecv.at[(oa * 4 + ob) * 2 + piece])

    def z_target(oa, ob):
        a_, b_ = m4(pa - oa), m4(pb - ob)
        yb = b_ + c * (a_ - b_)
        return dev(pa, pb, m4(z + 2 * lax.div(yb, 2) - 1))

    def zb_at(oa, ob):
        a_, b_ = m4(pa - oa), m4(pb - ob)
        return 256 + ((a_ * 2 + lax.rem(b_, 2)) * 2 + lax.div(b_, 2)) * 8

    def send_zb(oa, ob):
        go(remote(
            cur.at[pl.ds(base(oa, ob) + 4, 8)], cur.at[pl.ds(zb_at(oa, ob), 8)],
            zsend.at[oa * 4 + ob], zrecv.at[oa * 4 + ob], z_target(oa, ob),
        ))

    def got_zb(oa, ob):
        arrived(cur.at[pl.ds(zb_at(oa, ob), 8)], zrecv.at[oa * 4 + ob])

    def pattern_block(at):
        def pair(i, _):
            two = jnp.concatenate([cur[at + 2 * i], cur[at + 2 * i + 1]], axis=1)
            o = jnp.dot(rad[...], two, preferred_element_type=F32)
            buf[pl.ds(pl.multiple_of(2 * i * TB, TB), TB), :] = o[:, :128]
            buf[pl.ds(pl.multiple_of(2 * i * TB + TB, TB), TB), :] = o[:, 128:]
            return 0

        lax.fori_loop(0, 8, pair, 0)

        def turn(t, _):
            pat[t, pl.ds(at, 16), :] = buf[pl.ds(t, 16, stride=TB), :].astype(BF)
            return 0

        lax.fori_loop(0, TB, turn, 0, unroll=8)

    def pattern_main(oa, ob):
        pattern_block(base(oa, ob))

    def pattern_zb(oa, ob):
        got_zb(oa, ob)
        got_zb(oa, ob + 2)
        g = m4(pa - oa) * 2 + lax.rem(m4(pb - ob), 2)
        pattern_block(pl.multiple_of(256 + g * 16, 16))

    n_iota = lax.broadcasted_iota(jnp.int32, (384, 128), 0)
    lane = lax.broadcasted_iota(jnp.int32, (TB, 128), 1)

    def hot(ref, row):
        return jnp.where(n_iota == ref[pl.ds(row, 1), :], 1.0, 0.0).astype(BF)

    def mat_group(g):
        def two_rows(it, _):
            row = g * 8 + 2 * it
            classes = jnp.concatenate([hot(tid, row), hot(tid, row + 1)], axis=1)
            coef = jnp.dot(tt_t[...], classes, preferred_element_type=F32)
            for p in range(2):
                part = coef[:, p * 128 : (p + 1) * 128]
                both = jnp.concatenate(
                    [jnp.where(lane < 64, part, 0.0), jnp.where(lane < 64, 0.0, part)], axis=0
                ).astype(BF)
                placed = lax.dot_general(
                    both, hot(src, row + p), (((1,), (1,)), ((), ())), preferred_element_type=F32
                )
                r0 = (2 * it + p) * TB
                for h in range(2):
                    for q in range(3):
                        at = pl.multiple_of(q * 1536 + h * 8 * TB + r0, 8)
                        buf[pl.ds(at, TB), :] = placed[h * TB : (h + 1) * TB, q * 128 : (q + 1) * 128]
            return 0

        lax.fori_loop(0, 4, two_rows, 0)
        j0 = pl.multiple_of(g * 16, 16)

        def turn(t, _):
            for q in range(3):
                mat[t, pl.ds(j0, 16), q * 128 : (q + 1) * 128] = buf[
                    pl.ds(q * 1536 + t, 16, stride=TB), :
                ].astype(BF)
            return 0

        lax.fori_loop(0, TB, turn, 0, unroll=4)

    def mats(lo, hi):
        lax.fori_loop(lo, hi, lambda g, _: (mat_group(g), 0)[1], 0)

    keep.wait()
    arrived(cur.at[pl.ds(own0 + oc * 6, 6)], precv.at[0])
    go(remote(
        cur.at[pl.ds(own0, 4)], cur.at[pl.ds(own0 + 12, 4)],
        zsend.at[16], zrecv.at[16], z_target(0, 0),
    ))
    send_main(0, 0, 0, 12, a_up, 1, 0, 0)
    send_main(0, 0, 0, 12, a_dn, 3, 0, 0)
    send_main(0, 0, 0, 12, b_up, 0, 1, 0)
    send_main(0, 0, 0, 12, b_dn, 0, 3, 0)
    send_zb(0, 0)
    load_nb = pltpu.make_async_copy(nb_in, nb.at[pl.ds(c * 6, 6)], lsem.at[4])
    load_nb.start()
    go(remote(nb_in, nb.at[pl.ds(c * 6, 6)], psend.at[2], precv.at[2], partner))
    cur[384] = jnp.zeros((128, 128), BF)
    arrived(cur.at[pl.ds(own0 + 12, 4)], zrecv.at[16])
    send_main(0, 0, 12, 4, a_up, 1, 0, 1)
    send_main(0, 0, 12, 4, a_dn, 3, 0, 1)
    send_main(0, 0, 12, 4, b_up, 0, 1, 1)
    send_main(0, 0, 12, 4, b_dn, 0, 3, 1)
    mats(0, 1)

    def line_event(oa):
        send_main(oa, 0, 0, 16, b_up, oa, 1, 0)
        send_main(oa, 0, 0, 16, b_dn, oa, 3, 0)
        send_zb(oa, 0)

    for oa, lo, to, piece in ((1, 0, a_up, 0), (3, 8, a_dn, 1)):
        got_main(oa, 0, 0, 12, 0)
        got_main(oa, 0, 12, 4, 1)
        send_main(oa, 0, lo, 8, to, 2, 0, piece)
        line_event(oa)
    for ob, lo, to, piece in ((1, 0, b_up, 0), (3, 8, b_dn, 1)):
        got_main(0, ob, 0, 12, 0)
        got_main(0, ob, 12, 4, 1)
        send_main(0, ob, lo, 8, to, 0, 2, piece)
        send_zb(0, ob)
    load_rad.wait()
    mats(1, 3)
    pattern_main(0, 0)
    got_main(2, 0, 0, 8, 0)
    got_main(2, 0, 8, 8, 1)
    line_event(2)
    got_main(0, 2, 0, 8, 0)
    got_main(0, 2, 8, 8, 1)
    send_zb(0, 2)
    mats(3, 4)
    pattern_main(1, 0)
    pattern_main(3, 0)
    fill = {
        (1, 3): lambda: (mats(4, 6), pattern_main(0, 1)),
        (1, 2): lambda: (pattern_main(0, 3), pattern_main(2, 0), pattern_main(0, 2)),
        (3, 3): lambda: (mats(6, 8), pattern_main(1, 1)),
        (3, 2): lambda: (pattern_main(1, 3), pattern_main(1, 2), mats(8, 9)),
        (2, 3): lambda: (mats(9, 11), pattern_main(3, 1)),
        (2, 2): lambda: (pattern_main(3, 3), pattern_main(3, 2), mats(11, 12)),
    }
    for oa in (1, 3, 2):
        for ob, lo, to, piece in ((1, 0, b_up, 0), (3, 8, b_dn, 1)):
            got_main(oa, ob, 0, 16, 0)
            send_main(oa, ob, lo, 8, to, oa, 2, piece)
            send_zb(oa, ob)
        fill[(oa, 3)]()
        got_main(oa, 2, 0, 8, 0)
        got_main(oa, 2, 8, 8, 1)
        send_zb(oa, 2)
        fill[(oa, 2)]()
    pattern_main(2, 1)
    pattern_main(2, 3)
    pattern_main(2, 2)
    for oa in (0, 1, 3, 2):
        pattern_zb(oa, 0)
        pattern_zb(oa, 1)

    load_rcv.wait()
    k_at = lax.broadcasted_iota(jnp.int32, (8, 384), 1) + pb * 384
    width = jnp.zeros((8, 384), jnp.int32)
    for i in range(32):
        lo, hi = offs[i], offs[i + 1]
        width = jnp.where((k_at >= lo) & (k_at < hi), hi - lo, width)
    weight = 1536.0 / (32.0 * width.astype(F32))
    rw[...] = (rcv[...].astype(F32) * weight[:1]).astype(BF)
    load_ns.wait()
    arrived(nsv, precv.at[1])
    load_ns2 = pltpu.make_async_copy(nsv, ns_par, lsem.at[5])
    load_ns2.start()
    load_ns2.wait()
    load_nb.wait()
    arrived(nb.at[pl.ds(oc * 6, 6)], precv.at[2])

    def near_boxes(ns, first, lo, hi):
        def box(i, _):
            w = first + i
            total = jnp.zeros((128, 128), F32)
            for m in range(0, 26, 2):
                blocks = jnp.concatenate([nb[w, m], nb[w, m + 1]], axis=1)
                fields = jnp.concatenate([cur[ns[i, m]], cur[ns[i, m + 1]]], axis=0)
                total += jnp.dot(blocks, fields, preferred_element_type=F32)
            total += jnp.dot(nb[w, 26], cur[ns[i, 26]], preferred_element_type=F32)
            acc[w] = total
            return 0

        lax.fori_loop(lo, hi, box, 0)

    own_copies = []

    def chunk(k):
        def one(i, _):
            t = k * TCH + i
            buf[pl.ds(i, 192, stride=TCH), :] = jnp.dot(mat[t], pat[t], preferred_element_type=F32)
            return 0

        lax.fori_loop(0, TCH, one, 0)

        def pack(i, _):
            v = buf[pl.ds(pl.multiple_of(i * 128, 128), 128), :]
            tx[pl.ds(i * 8, 8), k * TCH : (k + 1) * TCH, :] = v.reshape(8, TCH, 128).astype(BF)
            return 0

        lax.fori_loop(0, 24, pack, 0)
        ts = pl.ds(k * TCH, TCH)
        there = pl.ds(pl.multiple_of(pa * TB + k * TCH, TCH), TCH)
        far = m4(pa + 2) * 48
        go(remote(tx.at[pl.ds(far, 24), ts], relay.at[0, k], rsend.at[k * 6 + 2], rrecv.at[k * 6 + 2], a_up))
        go(remote(tx.at[pl.ds(far + 24, 24), ts], relay.at[1, k], rsend.at[k * 6 + 3], rrecv.at[k * 6 + 3], a_dn))
        go(remote(tx.at[pl.ds(m4(pa + 1) * 48, 48), ts], rx.at[:, there], rsend.at[k * 6], rrecv.at[k * 6], a_up))
        go(remote(tx.at[pl.ds(m4(pa - 1) * 48, 48), ts], rx.at[:, there], rsend.at[k * 6 + 1], rrecv.at[k * 6 + 1], a_dn))
        own = pltpu.make_async_copy(tx.at[pl.ds(pa * 48, 48), ts], rx.at[:, there], lsem.at[6 + k])
        own.start()
        own_copies.append(own)

    def rx_at(a_, k):
        return pl.ds(pl.multiple_of(a_ * TB + k * TCH, TCH), TCH)

    def forward(k):
        arrived(relay.at[0, k], rrecv.at[k * 6 + 2])
        go(remote(relay.at[0, k], rx.at[pl.ds(0, 24), rx_at(m4(pa - 1), k)],
                  rsend.at[k * 6 + 4], rrecv.at[k * 6 + 4], a_up))
        arrived(relay.at[1, k], rrecv.at[k * 6 + 3])
        go(remote(relay.at[1, k], rx.at[pl.ds(24, 24), rx_at(m4(pa + 1), k)],
                  rsend.at[k * 6 + 5], rrecv.at[k * 6 + 5], a_dn))

    chunk(0)
    chunk(1)
    forward(0)
    chunk(2)
    near_boxes(ns_own, c * 6, 0, 2)
    forward(1)
    chunk(3)
    near_boxes(ns_own, c * 6, 2, 4)
    forward(2)
    chunk(4)
    near_boxes(ns_own, c * 6, 4, 6)
    forward(3)
    chunk(5)
    near_boxes(ns_par, oc * 6, 0, 3)
    forward(4)
    near_boxes(ns_par, oc * 6, 3, 6)
    forward(5)
    for k in range(NCH):
        own_copies[k].wait()
        arrived(rx.at[:, rx_at(m4(pa - 1), k)], rrecv.at[k * 6])
        arrived(rx.at[:, rx_at(m4(pa + 1), k)], rrecv.at[k * 6 + 1])
        arrived(rx.at[pl.ds(0, 24), rx_at(m4(pa + 2), k)], rrecv.at[k * 6 + 4])
        arrived(rx.at[pl.ds(24, 24), rx_at(m4(pa + 2), k)], rrecv.at[k * 6 + 5])

    def contract(b_, put):
        def pair(i, _):
            j = b_ * 12 + 2 * i
            two = jnp.concatenate([rx[j], rx[j + 1]], axis=1)
            o = jnp.dot(rw[...], two, preferred_element_type=F32)
            put(2 * i, o[:, :128])
            put(2 * i + 1, o[:, 128:])
            return 0

        lax.fori_loop(0, 6, pair, 0)

    def put_ps(slot):
        def put(w, v):
            ps[slot, w] = v.astype(BF)

        return put

    def put_acc(w, v):
        acc[w] = acc[w] + v

    for o, to in ((2, b_far), (1, b_up), (3, b_dn)):
        contract(m4(pb + o), put_ps(o - 1))
        go(remote(ps.at[o - 1], pr.at[o - 1], ssend.at[o - 1], srecv.at[o - 1], to))
    contract(pb, put_acc)
    for o in (1, 3, 2):
        arrived(pr.at[o - 1], srecv.at[o - 1])

    def finish(first, slot):
        def one(i, _):
            w = first + i
            total = acc[w] + pr[0, w].astype(F32) + pr[1, w].astype(F32) + pr[2, w].astype(F32)
            fin[slot, i] = total.astype(BF)
            return 0

        lax.fori_loop(0, 6, one, 0)

    mine = pl.ds(pl.multiple_of(c * 128, 128), 128)
    theirs = pl.ds(pl.multiple_of(oc * 128, 128), 128)
    finish(oc * 6, 1)
    go(remote(fin.at[1], out.at[:, :, mine], psend.at[3], precv.at[3], partner))
    finish(c * 6, 0)
    write = pltpu.make_async_copy(fin.at[0], out.at[:, :, mine], lsem.at[12])
    write.start()
    write.wait()
    arrived(out.at[:, :, theirs], precv.at[3])
    for copy in pending:
        copy.wait_send()


def slots_of(s, swap, g):
    halo = (s < 96) | (s >= 288)
    i = jnp.where(s < 96, s + 96, jnp.where(s >= 288, s - 288, s - 96))
    chip = lax.shift_right_arithmetic(i * 5462, 16)
    w = i - 12 * chip
    y = lax.shift_right_arithmetic(chip, 2)
    x = chip & 3
    a = jnp.where(swap, y, x)
    b = jnp.where(swap, x, y)
    near_slot = (a * 4 + b) * 16 + w
    far_slot = 256 + ((a * 2 + (b & 1)) * 2 + (b >> 1)) * 8 + (w - 4)
    slot = jnp.where(halo, jnp.where(w < 4, near_slot + 12, far_slot), near_slot)
    gone = (s < 0) | ((g == 0) & (s < 96)) | ((g == 3) & (s >= 288))
    return jnp.where(gone, -1, slot)


def shards(currents, radiate, receive, transfer_table, near_blocks, dir_offsets, trans_src, trans_tid, near_src):
    d = lax.axis_index("dir")
    g = lax.axis_index("region")
    swap = (d & 1) == 1
    x, y = (d >> 1) & 3, d >> 3
    pa, pb = jnp.where(swap, y, x), jnp.where(swap, x, y)
    band = pb * 4 + pa
    tt_t = lax.dynamic_slice_in_dim(transfer_table, band * TB, TB, 1).T
    tt_t = jnp.pad(tt_t, ((0, 0), (0, 384 - tt_t.shape[1])))

    def paired(v):
        v = v.reshape(4, 4, 12, 48)
        v = jnp.where(swap, v, v.transpose(1, 0, 2, 3)).reshape(12, 2, 8, 48)
        v = jnp.pad(v, ((0, 0), (0, 0), (0, 0), (0, 16)), constant_values=-1)
        return jnp.concatenate([v[:, 0], v[:, 1]], axis=-1).reshape(96, 128)

    src = paired(slots_of(trans_src[0], swap, g))
    tid = paired(trans_tid[0])
    near = near_src[0]
    near = jnp.where(near < 0, -1, near + 48)

    def near_slots(turned):
        v = slots_of(near, turned, g)
        v = jnp.where(v < 0, 384, v)
        return jnp.pad(v, ((0, 2), (0, 101)), constant_values=384)

    nsl = jnp.concatenate([near_slots(swap), near_slots(~swap)], axis=0)
    any_spec = pl.BlockSpec(memory_space=pl.ANY)
    vmem = pl.BlockSpec(memory_space=pltpu.VMEM)
    dma = pltpu.SemaphoreType.DMA
    out = pl.pallas_call(
        body,
        out_shape=jax.ShapeDtypeStruct((6, 128, 256), BF),
        in_specs=[any_spec] * 5 + [vmem] * 3 + [pl.BlockSpec(memory_space=pltpu.SMEM)],
        out_specs=any_spec,
        scratch_shapes=[
            pltpu.VMEM((385, 128, 128), BF),
            pltpu.VMEM((12, 27, 128, 128), BF),
            pltpu.VMEM((TB, 192, 384), BF),
            pltpu.VMEM((TB, 384, 128), BF),
            pltpu.VMEM((192, TB, 128), BF),
            pltpu.VMEM((48, 4 * TB, 128), BF),
            pltpu.VMEM((2, NCH, 24, TCH, 128), BF),
            pltpu.VMEM((3, 12, 128, 128), BF),
            pltpu.VMEM((3, 12, 128, 128), BF),
            pltpu.VMEM((12, 128, 128), F32),
            pltpu.VMEM((3 * 1536, 128), F32),
            pltpu.VMEM((TB, 128), BF),
            pltpu.VMEM((128, 384), BF),
            pltpu.VMEM((128, 384), BF),
            pltpu.VMEM((2, 6, 128, 128), BF),
            pltpu.VMEM((8, 128), jnp.int32),
            pltpu.SMEM((8, 128), jnp.int32),
            pltpu.SMEM((8, 128), jnp.int32),
            dma((13,)),
            dma((4,)),
            dma((4,)),
            dma((48,)),
            dma((32,)),
            dma((17,)),
            dma((17,)),
            dma((36,)),
            dma((36,)),
            dma((3,)),
            dma((3,)),
        ],
        compiler_params=pltpu.CompilerParams(
            collective_id=0, has_side_effects=True, vmem_limit_bytes=67043328
        ),
        name="fmm",
    )(currents[0], radiate, receive, near_blocks[0], nsl, tt_t, src, tid, dir_offsets)
    return out[None]


def solution(mesh):
    placed = (
        P("region", "dir", None, None),
        P(),
        P(),
        P(),
        P("region", "dir", None, None, None),
        P(),
        P("region", None, None),
        P("region", None, None),
        P("region", "dir", None),
    )
    return jax.shard_map(
        shards,
        mesh=mesh,
        in_specs=placed,
        out_specs=P("region", "dir", None, None),
        check_vma=False,
    )
```

time: 339 us -> 174 us (0.51); the launches traced: 334 us -> 173 us
  Pallas kernels: 0 us -> 163 us
  blocking collectives: 83.3 us -> 0 us
  waiting for transfers between devices: 74.6 us -> 0 us
  local copies, waits for them, and re-layouts: 70.2 us -> 5.25 us
  matrix products: 55.2 us -> 0 us
  starting transfers between devices: 21.7 us -> 0 us
  between operations: 13.6 us -> 0.13 us
  other arithmetic: 15.4 us -> 4.54 us
    pallas_call x0 -> x1, Pallas kernels: none -> 163 us  [shards(): pl.pallas_call(body, out_shape=jax.ShapeDtypeStruct((6, 128, 256), BF), i...]
    all_to_all x1 -> x0, blocking collectives: 83.3 us -> none  [shards(): lax.all_to_all(outgoing, 'dir', split_axis=1, concat_axis=0, tiled=True)]
    dot_general x5 -> x0, matrix products: 55.2 us -> none  [the longest x1 27.3 us: shards(): jnp.einsum('jsn,nt->tjs', pair_hot, coef_used, preferred_element_type=jnp...]
    all_to_all x1 -> x0, waiting for transfers between devices: 41.5 us -> none  [shards(): lax.all_to_all(translated, 'dir', split_axis=0, concat_axis=2, tiled=True)]
    ppermute x4 -> x0, waiting for transfers between devices: 32.4 us -> none  [the longest x2 28.1 us: padded(): after = lax.ppermute(initial, axis, down)]
    gather x2 -> x0, local copies, waits for them, and re-layouts: 27.9 us -> none  [shards(): picked = jnp.take(near_ext, jnp.maximum(near_here, 0), axis=0)]
    ppermute x4 -> x0, starting transfers between devices: 14.5 us -> none  [the longest x2 11.9 us: padded(): before = lax.ppermute(last, axis, up)]
    convert_element_type x2 -> x0, local copies, waits for them, and re-layouts: 13.8 us -> none  [the longest x1 7.17 us: shards(): translated = jnp.einsum('tjs,str->jtr', matrix, extended, preferred_eleme...]
  transfers between devices with their start and end apart: 6 -> 0, of which waited for: 5 -> 0; matrix products, arithmetic and copies ran while one was open for 25% -> 0% of each run, Pallas kernels for 0% -> 0%
where the time goes in v1:
time: 174 us; the launch traced here: 173 us
  Pallas kernels  163 us (94%)
  local copies, waits for them, and re-layouts  5.25 us (3%)
  other arithmetic  4.54 us (3%)
    pallas_call x1, Pallas kernels, shards(): pl.pallas_call(body, out_shape=jax.ShapeDtypeStruct((6, 128, 256), BF), i...  163 us

profile of v1, /device:TPU:1, one launch (start us, length us, event | category | flops | bytes accessed | tf_op | source)
XLA Modules:
  0.0 173.2 jit_solution(10682973937865295156)
XLA Ops:
  0.0 1.0 constant_dynamic-slice_fusion
  1.0 0.1 copy.39
  1.1 0.6 pad.20.tt_t
  1.8 0.8 broadcast_add_fusion
  2.6 0.1 copy.33
  2.7 0.1 copy.34
  2.8 0.1 copy.35
  2.9 0.8 broadcast_compare_fusion.2
  3.8 0.1 copy.32
  3.9 0.1 copy.30
  4.1 0.1 copy.31
  4.2 0.2 select_select_fusion
  4.4 0.9 copy.37
  5.4 0.7 pad_add_fusion.1.tid
  6.1 0.7 pad_add_fusion.src
  6.8 0.7 compare_select_fusion.1
  7.5 0.6 select_add_fusion.nsl_in
  8.2 163.3 %fmm.1 = bf16[6,128,256]{2,1,0:T(8,128)(2,1)} custom-call(bf16[6,128,256]{2,1,0:T(8,128)(2,1)} %bitcast.82, bf16[1536,128]{1,0:T(8,128)(2,1)} %rad_in.1, bf16[128,1536]{1,0:T(8,128)(2,1)} %rcv_in.1, bf16[6,27,128,128]{3,2,1,0:T(8,128)(2,1)} %bitcast.80, s32[16,128]{1,0:T(8,128)} %select_add_fusion.nsl_in, bf16[96,384]{1,0:T(8,128)(2,1)} %pad.20.tt_t, ...), custom_call_target="tpu_custom_call" | custom-call | tf_op jit(solution)/shard_map/fmm/pallas_call | solution.py:451
  171.5 1.8 %copy.53 = bf16[1,6,128,256]{3,2,1,0:T(8,128)(2,1)} copy(bf16[1,6,128,256]{3,2,1,0:T(8,128)(2,1)} %bitcast.81) | data formatting | bytes 786432
  (12 shorter events, 0.2 us)

commit v2 on v0

v2 whole, which is shorter than its diff:
```python
import jax
import jax.numpy as jnp
from jax import lax
from jax.experimental import pallas as pl
from jax.experimental.pallas import tpu as pltpu
from jax.sharding import PartitionSpec as P

MESH = pl.DeviceIdType.MESH
BF = jnp.bfloat16
F32 = jnp.float32
TB = 96
NCH = 6
TCH = TB // 3


def m4(v):
    return lax.rem(v + 8, 4)


def body(
    cur_in, rad_in, rcv_in, nb_in, near_in, tt_in, src_in, tid_in, offs_in, out,
    cur, nb, mat, pat, tx, rx, relay, ps, pr, acc, bpat, bmat, btr, rad, rcv, rw, fin,
    near_v, near_m, ns, tts, wide, tt_t, sraw, stage, src, tid, offs,
    lsem, psend, precv, asend, arecv, zsend, zrecv, rsend, rrecv, ssend, srecv,
):
    d = lax.axis_index("dir")
    z = lax.axis_index("region")
    c = lax.rem(d, 2)
    chip = lax.div(d, 2)
    x = lax.rem(chip, 4)
    y = lax.div(chip, 4)
    pa = x + c * (y - x)
    pb = y + c * (x - y)
    oc = 1 - c

    def dev(a, b, zz=None):
        xx = a + c * (b - a)
        yy = b + c * (a - b)
        return ((yy * 4 + xx) * 2 + c, z if zz is None else zz)

    partner = (d + 1 - 2 * c, z)
    a_up, a_dn = dev(m4(pa + 1), pb), dev(m4(pa - 1), pb)
    b_up, b_dn = dev(pa, m4(pb + 1)), dev(pa, m4(pb - 1))
    b_far = dev(pa, m4(pb + 2))
    z_up, z_dn = dev(pa, pb, m4(z + 1)), dev(pa, pb, m4(z - 1))

    barrier = pltpu.get_barrier_semaphore()
    for peer in (z_up, z_dn, b_far, a_up, a_dn, b_up, b_dn, partner):
        pl.semaphore_signal(barrier, inc=1, device_id=peer, device_id_type=MESH)

    lane0 = pl.multiple_of(c * 128, 128)
    own_half = cur_in.at[:, :, pl.ds(lane0, 128)]

    def base(oa, ob):
        return pl.multiple_of((m4(pa - oa) * 4 + m4(pb - ob)) * 16, 16)

    own0 = base(0, 0)
    loads = {}

    def load(name, src_ref, dst_ref):
        loads[name] = pltpu.make_async_copy(src_ref, dst_ref, lsem.at[len(loads)])
        loads[name].start()

    load("keep", own_half, cur.at[pl.ds(own0, 6)])
    load("src", src_in, sraw.at[0])
    load("tid", tid_in, sraw.at[1])
    load("tt", tt_in.at[:, pl.ds(pl.multiple_of(pb * 384, 128), 384)], tts)
    load("rad", rad_in.at[pl.ds(pl.multiple_of((pb * 4 + pa) * TB, 16), TB)], rad)
    load("rcv", rcv_in.at[:, pl.ds(pl.multiple_of(pb * 384, 128), 384)], rcv)
    load("near", near_in, near_v.at[0])
    load("offs", offs_in, offs)

    pl.semaphore_wait(barrier, 8)
    pending = []

    def remote(src_ref, dst_ref, send, recv, to):
        return pltpu.make_async_remote_copy(
            src_ref=src_ref, dst_ref=dst_ref, send_sem=send, recv_sem=recv,
            device_id=to, device_id_type=MESH,
        )

    def go(copy):
        copy.start()
        pending.append(copy)

    def arrived(ref, sem):
        remote(ref, ref, psend.at[0], sem, partner).wait_recv()

    count = [0]

    def send_main(oa, ob, lo, n, to, ra, rb, piece, origin=None):
        part = cur.at[pl.ds(base(oa, ob) + lo, n)]
        go(remote(part if origin is None else origin, part,
                  asend.at[count[0]], arecv.at[(ra * 4 + rb) * 3 + piece], to))
        count[0] += 1

    def got_main(oa, ob, lo, n, piece):
        arrived(cur.at[pl.ds(base(oa, ob) + lo, n)], arecv.at[(oa * 4 + ob) * 3 + piece])

    def z_target(oa, ob):
        a_, b_ = m4(pa - oa), m4(pb - ob)
        yb = b_ + c * (a_ - b_)
        return dev(pa, pb, m4(z + 2 * lax.div(yb, 2) - 1))

    def zb_at(oa, ob):
        a_, b_ = m4(pa - oa), m4(pb - ob)
        return 256 + ((a_ * 2 + lax.rem(b_, 2)) * 2 + lax.div(b_, 2)) * 8

    def send_zb(oa, ob):
        go(remote(
            cur.at[pl.ds(base(oa, ob) + 4, 8)], cur.at[pl.ds(zb_at(oa, ob), 8)],
            zsend.at[oa * 4 + ob], zrecv.at[oa * 4 + ob], z_target(oa, ob),
        ))

    def got_zb(oa, ob):
        arrived(cur.at[pl.ds(zb_at(oa, ob), 8)], zrecv.at[oa * 4 + ob])

    def send_own(lo, n, piece, origin=None):
        send_main(0, 0, lo, n, a_up, 1, 0, piece, origin)
        send_main(0, 0, lo, n, a_dn, 3, 0, piece, origin)
        send_main(0, 0, lo, n, b_up, 0, 1, piece, origin)
        send_main(0, 0, lo, n, b_dn, 0, 3, piece, origin)

    go(remote(
        cur_in.at[:, :, pl.ds(pl.multiple_of(oc * 128, 128), 128)],
        cur.at[pl.ds((pb * 4 + pa) * 16 + 6, 6)], psend.at[0], precv.at[0], partner,
    ))
    go(remote(
        cur_in.at[pl.ds(0, 4), :, pl.ds(lane0, 128)], cur.at[pl.ds(own0 + 12, 4)],
        zsend.at[16], zrecv.at[16], z_target(0, 0),
    ))
    send_own(0, 6, 0, own_half)
    go(remote(near_in, near_v.at[1], psend.at[1], precv.at[1], partner))
    loads["keep"].wait()
    arrived(cur.at[pl.ds(own0 + 6, 6)], precv.at[0])
    send_own(6, 6, 1)
    send_zb(0, 0)
    arrived(cur.at[pl.ds(own0 + 12, 4)], zrecv.at[16])
    send_own(12, 4, 2)
    load("nb", nb_in, nb.at[pl.ds(0, 6)])
    go(remote(nb_in, nb.at[pl.ds(6, 6)], psend.at[2], precv.at[2], partner))
    cur[384] = jnp.zeros((128, 128), BF)

    def slot_of(s):
        halo = (s < 96) | (s >= 288)
        i = jnp.where(s < 96, s + 96, jnp.where(s >= 288, s - 288, s - 96))
        box_chip = lax.shift_right_arithmetic(i * 5462, 16)
        p = i - 12 * box_chip - 6 * c
        p = jnp.where(p < 0, p + 12, p)
        by = lax.shift_right_arithmetic(box_chip, 2)
        bx = box_chip - 4 * by
        a = bx + c * (by - bx)
        b = by + c * (bx - by)
        b_hi = lax.shift_right_arithmetic(b, 1)
        main = (a * 4 + b) * 16 + p
        beyond = 256 + ((a * 2 + b - 2 * b_hi) * 2 + b_hi) * 8 + (p - 4)
        slot = jnp.where(halo, jnp.where(p < 4, main + 12, beyond), main)
        low = jnp.where(z == 0, 96, 0)
        high = jnp.where(z == 3, 288, 384)
        return jnp.where((s < low) | (s >= high), -1, slot)

    def table(values, ref):
        stage[...] = jnp.full((128, 256), -1.0, F32)
        stage[0:48, 0:192] = values
        stage[64:112, 0:192] = values
        ref[0:128, :] = jnp.transpose(stage[:, 0:128])
        ref[128:256, :] = jnp.transpose(stage[:, 128:256])

    loads["src"].wait()
    table(slot_of(sraw[0]).astype(F32), src)
    loads["tid"].wait()
    table(sraw[1].astype(F32), tid)
    loads["tt"].wait()
    wide[...] = jnp.zeros((384, 384), F32)
    wide[0:316, :] = tts[...].astype(F32)
    tt_t[...] = jnp.transpose(wide[...]).astype(BF)
    loads["rad"].wait()

    def pattern_block(at):
        def pair(i, _):
            two = jnp.concatenate([cur[at + 2 * i], cur[at + 2 * i + 1]], axis=1)
            o = jnp.dot(rad[...], two, preferred_element_type=F32)
            bpat[2 * i] = o[:, :128].astype(BF)
            bpat[2 * i + 1] = o[:, 128:].astype(BF)
            return 0

        lax.fori_loop(0, 8, pair, 0)

        def turn(i, _):
            t0 = pl.multiple_of(i * 16, 16)
            pat[pl.ds(t0, 16), pl.ds(at, 16), :] = jnp.swapaxes(bpat[:, pl.ds(t0, 16), :], 0, 1)
            return 0

        lax.fori_loop(0, TB // 16, turn, 0, unroll=2)

    def patterns(*blocks):
        for oa, ob in blocks:
            pattern_block(base(oa, ob))

    def pattern_zb(oa, ob):
        got_zb(oa, ob)
        got_zb(oa, ob + 2)
        g = m4(pa - oa) * 2 + lax.rem(m4(pb - ob), 2)
        pattern_block(pl.multiple_of(256 + g * 16, 16))

    n_iota = lax.broadcasted_iota(jnp.int32, (384, 128), 0).astype(F32)
    lane = lax.broadcasted_iota(jnp.int32, (TB, 128), 1)

    def box_row(jp):
        group = lax.div(jp, 24)
        rest = jp - group * 24
        second = lax.div(rest, 12)
        p = rest - second * 12
        half = lax.div(group, 4)
        a_ = group - 4 * half
        b_ = m4(pb + jnp.where(half == 0, 2 - second, 3 - 3 * second))
        chip_ = (b_ + c * (a_ - b_)) * 4 + a_ + c * (b_ - a_)
        return chip_ * 12 + lax.rem(p + 6 * c, 12)

    def hot(ref, lo, hi):
        row = jnp.where(lane[:1] < 64, ref[pl.ds(lo, 1), :], ref[pl.ds(hi, 1), :])
        return jnp.where(n_iota == row, 1.0, 0.0).astype(BF)

    def mat_group(g):
        def two_rows(it, _):
            rows = [(box_row(g * 16 + 2 * it + p), box_row(g * 16 + 8 + 2 * it + p)) for p in range(2)]
            classes = jnp.concatenate([hot(tid, *rows[0]), hot(tid, *rows[1])], axis=1)
            coef = jnp.dot(
                tt_t[pl.ds(pl.multiple_of(pa * TB, 16), TB), :], classes, preferred_element_type=F32
            )
            for p in range(2):
                part = coef[:, p * 128 : (p + 1) * 128]
                both = jnp.concatenate(
                    [jnp.where(lane < 64, part, 0.0), jnp.where(lane < 64, 0.0, part)], axis=0
                ).astype(BF)
                placed = lax.dot_general(
                    both, hot(src, *rows[p]), (((1,), (1,)), ((), ())), preferred_element_type=F32
                )
                for h in range(2):
                    bmat[h * 8 + 2 * it + p] = placed[h * TB : (h + 1) * TB].astype(BF)
            return 0

        lax.fori_loop(0, 4, two_rows, 0)
        j0 = pl.multiple_of(g * 16, 16)

        def turn(i, _):
            t0 = pl.multiple_of(i * 16, 16)
            for q in range(3):
                lanes = slice(q * 128, (q + 1) * 128)
                mat[pl.ds(t0, 16), pl.ds(j0, 16), lanes] = jnp.swapaxes(bmat[:, pl.ds(t0, 16), lanes], 0, 1)
            return 0

        lax.fori_loop(0, TB // 16, turn, 0)

    def mats(lo, hi):
        lax.fori_loop(lo, hi, lambda g, _: (mat_group(g), 0)[1], 0)

    def line_event(oa):
        send_main(oa, 0, 0, 16, b_up, oa, 1, 0)
        send_main(oa, 0, 0, 16, b_dn, oa, 3, 0)

    for oa, ob in ((1, 0), (3, 0), (0, 1), (0, 3)):
        got_main(oa, ob, 0, 6, 0)
        got_main(oa, ob, 6, 6, 1)
        if (oa, ob) == (1, 0):
            send_main(1, 0, 0, 8, a_up, 2, 0, 0)
        if (oa, ob) == (0, 1):
            send_main(0, 1, 0, 8, b_up, 0, 2, 0)
        send_zb(oa, ob)
    got_main(3, 0, 12, 4, 2)
    send_main(3, 0, 8, 8, a_dn, 2, 0, 1)
    line_event(3)
    got_main(1, 0, 12, 4, 2)
    line_event(1)
    got_main(0, 3, 12, 4, 2)
    send_main(0, 3, 8, 8, b_dn, 0, 2, 1)
    got_main(0, 1, 12, 4, 2)
    mats(0, 1)
    patterns((0, 0))

    def halves(oa, ob):
        got_main(oa, ob, 0, 8, 0)
        got_main(oa, ob, 8, 8, 1)
        send_zb(oa, ob)

    def ring_event(oa):
        for ob, lo, to, piece in ((1, 0, b_up, 0), (3, 8, b_dn, 1)):
            got_main(oa, ob, 0, 16, 0)
            send_main(oa, ob, lo, 8, to, oa, 2, piece)
            send_zb(oa, ob)

    halves(2, 0)
    line_event(2)
    mats(1, 2)
    patterns((1, 0))
    ring_event(3)
    mats(2, 3)
    patterns((3, 0), (2, 0))
    ring_event(1)
    halves(0, 2)
    mats(3, 5)
    patterns((0, 1), (0, 3))
    ring_event(2)
    mats(5, 7)
    patterns((3, 1), (3, 3), (0, 2))
    halves(3, 2)
    mats(7, 9)
    patterns((1, 1), (1, 3))
    halves(1, 2)
    mats(9, 12)
    patterns((2, 1), (2, 3), (3, 2), (1, 2))
    halves(2, 2)
    patterns((2, 2))
    for oa, ob in ((0, 0), (0, 1), (3, 1), (1, 1), (3, 0), (1, 0), (2, 1), (2, 0)):
        pattern_zb(oa, ob)

    own_copies = []

    def chunk(h, k):
        n = h * 3 + k
        j0 = h * 96

        def one(i, _):
            t = k * TCH + i
            btr[i] = jnp.dot(mat[t, j0 : j0 + 96, :], pat[t], preferred_element_type=F32).astype(BF)
            return 0

        lax.fori_loop(0, TCH, one, 0, unroll=2)

        def pack(i, _):
            r0 = pl.multiple_of(lax.rem(i, 6) * 16, 16)
            t0 = pl.multiple_of(lax.div(i, 6) * 16, 16)
            tx[pl.ds(j0 + r0, 16), pl.ds(k * TCH + t0, 16), :] = jnp.swapaxes(
                btr[pl.ds(t0, 16), pl.ds(r0, 16), :], 0, 1
            )
            return 0

        lax.fori_loop(0, 12, pack, 0, unroll=2)
        ts = pl.ds(k * TCH, TCH)
        here = pl.ds(h * 24, 24)
        there = rx_at(pa, k)
        far = j0 + m4(pa + 2) * 24
        go(remote(tx.at[pl.ds(far, 12), ts], relay.at[0, n], rsend.at[n * 6 + 2], rrecv.at[n * 6 + 2], a_up))
        go(remote(tx.at[pl.ds(far + 12, 12), ts], relay.at[1, n], rsend.at[n * 6 + 3], rrecv.at[n * 6 + 3], a_dn))
        go(remote(tx.at[pl.ds(j0 + m4(pa + 1) * 24, 24), ts], rx.at[here, there], rsend.at[n * 6], rrecv.at[n * 6], a_up))
        go(remote(tx.at[pl.ds(j0 + m4(pa - 1) * 24, 24), ts], rx.at[here, there], rsend.at[n * 6 + 1], rrecv.at[n * 6 + 1], a_dn))
        own = pltpu.make_async_copy(tx.at[pl.ds(j0 + pa * 24, 24), ts], rx.at[here, there], lsem.at[10 + n])
        own.start()
        own_copies.append(own)

    def rx_at(a_, k):
        return pl.ds(pl.multiple_of(a_ * TB + k * TCH, TCH), TCH)

    def forward(h, k):
        n = h * 3 + k
        arrived(relay.at[0, n], rrecv.at[n * 6 + 2])
        go(remote(relay.at[0, n], rx.at[pl.ds(h * 24, 12), rx_at(m4(pa - 1), k)],
                  rsend.at[n * 6 + 4], rrecv.at[n * 6 + 4], a_up))
        arrived(relay.at[1, n], rrecv.at[n * 6 + 3])
        go(remote(relay.at[1, n], rx.at[pl.ds(h * 24 + 12, 12), rx_at(m4(pa + 1), k)],
                  rsend.at[n * 6 + 5], rrecv.at[n * 6 + 5], a_dn))

    def all_here(h):
        here = pl.ds(h * 24, 24)
        for k in range(3):
            n = h * 3 + k
            own_copies[n].wait()
            arrived(rx.at[here, rx_at(m4(pa - 1), k)], rrecv.at[n * 6])
            arrived(rx.at[here, rx_at(m4(pa + 1), k)], rrecv.at[n * 6 + 1])
            arrived(rx.at[pl.ds(h * 24, 12), rx_at(m4(pa + 2), k)], rrecv.at[n * 6 + 4])
            arrived(rx.at[pl.ds(h * 24 + 12, 12), rx_at(m4(pa + 2), k)], rrecv.at[n * 6 + 5])

    def near_boxes(which, lo, hi):
        def box(i, _):
            w = which * 6 + i
            total = jnp.zeros((128, 128), F32)
            for m in range(0, 26, 2):
                blocks = jnp.concatenate([nb[w, m], nb[w, m + 1]], axis=1)
                fields = jnp.concatenate([cur[ns[which, i, 0, m]], cur[ns[which, i, 0, m + 1]]], axis=0)
                total += jnp.dot(blocks, fields, preferred_element_type=F32)
            total += jnp.dot(nb[w, 26], cur[ns[which, i, 0, 26]], preferred_element_type=F32)
            acc[w] = total
            return 0

        lax.fori_loop(lo, hi, box, 0)

    def contract(group, put):
        def pair(i, _):
            j = group * 12 + 2 * i
            two = jnp.concatenate([rx[j], rx[j + 1]], axis=1)
            o = jnp.dot(rw[...], two, preferred_element_type=F32)
            put(2 * i, o[:, :128])
            put(2 * i + 1, o[:, 128:])
            return 0

        lax.fori_loop(0, 6, pair, 0)

    def partial_to(group, o, to):
        def put(w, v):
            ps[o - 1, w] = v.astype(BF)

        contract(group, put)
        go(remote(ps.at[o - 1], pr.at[o - 1], ssend.at[o - 1], srecv.at[o - 1], to))

    def put_acc(w, v):
        acc[w] = acc[w] + v

    chunk(0, 0)
    chunk(0, 1)
    forward(0, 0)
    chunk(0, 2)
    forward(0, 1)
    chunk(1, 0)
    loads["rcv"].wait()
    loads["offs"].wait()
    k_at = lax.broadcasted_iota(jnp.int32, (8, 384), 1) + pb * 384
    width = jnp.zeros((8, 384), jnp.int32)
    for i in range(32):
        lo, hi = offs[i], offs[i + 1]
        width = jnp.where((k_at >= lo) & (k_at < hi), hi - lo, width)
    weight = 1536.0 / (32.0 * width.astype(F32))
    rw[...] = (rcv[...].astype(F32) * weight[:1]).astype(BF)
    loads["near"].wait()
    arrived(near_v.at[1], precv.at[1])
    near_s = near_v[...]
    near_s = slot_of(jnp.where(near_s < 0, -1, near_s + 48))
    near_m[...] = jnp.where(near_s < 0, 384, near_s)
    forward(0, 2)
    load("ns", near_m, ns)
    chunk(1, 1)
    loads["ns"].wait()
    loads["nb"].wait()
    near_boxes(0, 0, 2)
    forward(1, 0)
    chunk(1, 2)
    all_here(0)
    partial_to(0, 2, b_far)
    partial_to(1, 1, b_up)
    forward(1, 1)
    near_boxes(0, 2, 5)
    forward(1, 2)
    near_boxes(0, 5, 6)
    arrived(nb.at[pl.ds(6, 6)], precv.at[2])
    near_boxes(1, 0, 6)
    all_here(1)
    partial_to(2, 3, b_dn)
    contract(3, put_acc)
    for o in (2, 1, 3):
        arrived(pr.at[o - 1], srecv.at[o - 1])

    def finish(which):
        def one(i, _):
            w = which * 6 + i
            total = acc[w] + pr[0, w].astype(F32) + pr[1, w].astype(F32) + pr[2, w].astype(F32)
            fin[which, i] = total.astype(BF)
            return 0

        lax.fori_loop(0, 6, one, 0)

    mine = pl.ds(lane0, 128)
    theirs = pl.ds(pl.multiple_of(oc * 128, 128), 128)
    finish(1)
    go(remote(fin.at[1], out.at[:, :, mine], psend.at[3], precv.at[3], partner))
    finish(0)
    write = pltpu.make_async_copy(fin.at[0], out.at[:, :, mine], lsem.at[16])
    write.start()
    write.wait()
    arrived(out.at[:, :, theirs], precv.at[3])
    for copy in pending:
        copy.wait_send()


def shards(currents, radiate, receive, transfer_table, near_blocks, dir_offsets, trans_src, trans_tid, near_src):
    any_spec = pl.BlockSpec(memory_space=pl.ANY)
    dma = pltpu.SemaphoreType.DMA
    out = pl.pallas_call(
        body,
        out_shape=jax.ShapeDtypeStruct((6, 128, 256), BF),
        in_specs=[any_spec] * 9,
        out_specs=any_spec,
        scratch_shapes=[
            pltpu.VMEM((385, 128, 128), BF),
            pltpu.VMEM((12, 27, 128, 128), BF),
            pltpu.VMEM((TB, 192, 384), BF),
            pltpu.VMEM((TB, 384, 128), BF),
            pltpu.VMEM((192, TB, 128), BF),
            pltpu.VMEM((48, 4 * TB, 128), BF),
            pltpu.VMEM((2, NCH, 12, TCH, 128), BF),
            pltpu.VMEM((3, 12, 128, 128), BF),
            pltpu.VMEM((3, 12, 128, 128), BF),
            pltpu.VMEM((12, 128, 128), F32),
            pltpu.VMEM((16, TB, 128), BF),
            pltpu.VMEM((16, TB, 384), BF),
            pltpu.VMEM((TCH, 96, 128), BF),
            pltpu.VMEM((TB, 128), BF),
            pltpu.VMEM((128, 384), BF),
            pltpu.VMEM((128, 384), BF),
            pltpu.VMEM((2, 6, 128, 128), BF),
            pltpu.VMEM((2, 6, 1, 27), jnp.int32),
            pltpu.VMEM((2, 6, 1, 27), jnp.int32),
            pltpu.SMEM((2, 6, 1, 27), jnp.int32),
            pltpu.VMEM((316, 384), BF),
            pltpu.VMEM((384, 384), F32),
            pltpu.VMEM((384, 384), BF),
            pltpu.VMEM((2, 48, 192), jnp.int32),
            pltpu.VMEM((128, 256), F32),
            pltpu.VMEM((256, 128), F32),
            pltpu.VMEM((256, 128), F32),
            pltpu.SMEM((33,), jnp.int32),
            dma((17,)),
            dma((4,)),
            dma((4,)),
            dma((48,)),
            dma((48,)),
            dma((17,)),
            dma((17,)),
            dma((36,)),
            dma((36,)),
            dma((3,)),
            dma((3,)),
        ],
        compiler_params=pltpu.CompilerParams(
            collective_id=0, has_side_effects=True, vmem_limit_bytes=67043328
        ),
        name="fmm",
    )(
        currents[0], radiate, receive, near_blocks[0], jnp.swapaxes(near_src, 0, 1), transfer_table,
        jnp.swapaxes(trans_src[0], 0, 1), jnp.swapaxes(trans_tid[0], 0, 1), dir_offsets,
    )
    return out[None]


def solution(mesh):
    placed = (
        P("region", "dir", None, None),
        P(),
        P(),
        P(),
        P("region", "dir", None, None, None),
        P(),
        P("region", None, None),
        P("region", None, None),
        P("region", "dir", None),
    )
    return jax.shard_map(
        shards,
        mesh=mesh,
        in_specs=placed,
        out_specs=P("region", "dir", None, None),
        check_vma=False,
    )
```

time: 339 us -> 139 us (0.41); the launches traced: 334 us -> 139 us
  Pallas kernels: 0 us -> 137 us
  blocking collectives: 83.3 us -> 0 us
  waiting for transfers between devices: 74.6 us -> 0 us
  local copies, waits for them, and re-layouts: 70.2 us -> 1.77 us
  matrix products: 55.2 us -> 0 us
  starting transfers between devices: 21.7 us -> 0 us
  other arithmetic: 15.4 us -> 0 us
  between operations: 13.6 us -> 0.01 us
    pallas_call x0 -> x1, Pallas kernels: none -> 137 us  [shards(): pl.pallas_call(body, out_shape=jax.ShapeDtypeStruct((6, 128, 256), BF), i...]
    all_to_all x1 -> x0, blocking collectives: 83.3 us -> none  [shards(): lax.all_to_all(outgoing, 'dir', split_axis=1, concat_axis=0, tiled=True)]
    dot_general x5 -> x0, matrix products: 55.2 us -> none  [the longest x1 27.3 us: shards(): jnp.einsum('jsn,nt->tjs', pair_hot, coef_used, preferred_element_type=jnp...]
    all_to_all x1 -> x0, waiting for transfers between devices: 41.5 us -> none  [shards(): lax.all_to_all(translated, 'dir', split_axis=0, concat_axis=2, tiled=True)]
    ppermute x4 -> x0, waiting for transfers between devices: 32.4 us -> none  [the longest x2 28.1 us: padded(): after = lax.ppermute(initial, axis, down)]
    gather x2 -> x0, local copies, waits for them, and re-layouts: 27.9 us -> none  [shards(): picked = jnp.take(near_ext, jnp.maximum(near_here, 0), axis=0)]
    concatenate x1 -> x0, other arithmetic: 15.2 us -> none  [padded(): array = jnp.concatenate([before, array, after], axis=dim)]
    ppermute x4 -> x0, starting transfers between devices: 14.5 us -> none  [the longest x2 11.9 us: padded(): before = lax.ppermute(last, axis, up)]
  transfers between devices with their start and end apart: 6 -> 0, of which waited for: 5 -> 0; matrix products, arithmetic and copies ran while one was open for 25% -> 0% of each run, Pallas kernels for 0% -> 0%
where the time goes in v2:
time: 139 us
  Pallas kernels  137 us (99%)
  local copies, waits for them, and re-layouts  1.77 us (1%)
    pallas_call x1, Pallas kernels, shards(): pl.pallas_call(body, out_shape=jax.ShapeDtypeStruct((6, 128, 256), BF), i...  137 us

profile of v2, /device:TPU:1, one launch (start us, length us, event | category | flops | bytes accessed | tf_op | source)
XLA Modules:
  0.0 139.0 jit_solution(14573261425280719282)
XLA Ops:
  0.0 137.2 %fmm.1 = bf16[6,128,256]{2,1,0:T(8,128)(2,1)} custom-call(bf16[6,128,256]{2,1,0:T(8,128)(2,1)} %bitcast.12, bf16[1536,128]{1,0:T(8,128)(2,1)} %rad_in.1, bf16[128,1536]{1,0:T(8,128)(2,1)} %rcv_in.1, bf16[6,27,128,128]{3,2,1,0:T(8,128)(2,1)} %bitcast.10, s32[6,1,27]{2,1,0:T(1,128)} %bitcast.15, bf16[316,1536]{1,0:T(8,128)(2,1)} %tt_in.1, s32[48,192]{1,0:T(8,128)} %bitcast.13, ...), custom_call_target="tpu_custom_call" | custom-call | tf_op jit(solution)/shard_map/fmm/pallas_call | solution.py:476
  137.2 1.8 %copy.11 = bf16[1,6,128,256]{3,2,1,0:T(8,128)(2,1)} copy(bf16[1,6,128,256]{3,2,1,0:T(8,128)(2,1)} %bitcast.11) | data formatting | bytes 786432

commit v3 on v2

--- a/solution.py
+++ b/solution.py
@@ -19,7 +19,7 @@
 
 def body(
     cur_in, rad_in, rcv_in, nb_in, near_in, tt_in, src_in, tid_in, offs_in, out,
-    cur, nb, mat, pat, tx, rx, relay, ps, pr, acc, bpat, bmat, btr, rad, rcv, rw, fin,
+    cur, nb, mat, pat, tx, rx, relay, hop, ps, pr, acc, bpat, bmat, btr, rad, rcv, rw, fin,
     near_v, near_m, ns, tts, wide, tt_t, sraw, stage, src, tid, offs,
     lsem, psend, precv, asend, arecv, zsend, zrecv, rsend, rrecv, ssend, srecv,
 ):
@@ -41,18 +41,17 @@
     partner = (d + 1 - 2 * c, z)
     a_up, a_dn = dev(m4(pa + 1), pb), dev(m4(pa - 1), pb)
     b_up, b_dn = dev(pa, m4(pb + 1)), dev(pa, m4(pb - 1))
-    b_far = dev(pa, m4(pb + 2))
     z_up, z_dn = dev(pa, pb, m4(z + 1)), dev(pa, pb, m4(z - 1))
 
     barrier = pltpu.get_barrier_semaphore()
-    for peer in (z_up, z_dn, b_far, a_up, a_dn, b_up, b_dn, partner):
+    for peer in (z_up, z_dn, a_up, a_dn, b_up, b_dn, partner):
         pl.semaphore_signal(barrier, inc=1, device_id=peer, device_id_type=MESH)
 
     lane0 = pl.multiple_of(c * 128, 128)
     own_half = cur_in.at[:, :, pl.ds(lane0, 128)]
 
     def base(oa, ob):
-        return pl.multiple_of((m4(pa - oa) * 4 + m4(pb - ob)) * 16, 16)
+        return (m4(pa - oa) * 4 + m4(pb - ob)) * 18
 
     own0 = base(0, 0)
     loads = {}
@@ -70,7 +69,7 @@
     load("near", near_in, near_v.at[0])
     load("offs", offs_in, offs)
 
-    pl.semaphore_wait(barrier, 8)
+    pl.semaphore_wait(barrier, 7)
     pending = []
 
     def remote(src_ref, dst_ref, send, recv, to):
@@ -104,16 +103,16 @@
 
     def zb_at(oa, ob):
         a_, b_ = m4(pa - oa), m4(pb - ob)
-        return 256 + ((a_ * 2 + lax.rem(b_, 2)) * 2 + lax.div(b_, 2)) * 8
+        return 288 + ((a_ * 2 + lax.rem(b_, 2)) * 2 + lax.div(b_, 2)) * 6
 
     def send_zb(oa, ob):
         go(remote(
-            cur.at[pl.ds(base(oa, ob) + 4, 8)], cur.at[pl.ds(zb_at(oa, ob), 8)],
+            cur.at[pl.ds(base(oa, ob) + 6, 6)], cur.at[pl.ds(zb_at(oa, ob), 6)],
             zsend.at[oa * 4 + ob], zrecv.at[oa * 4 + ob], z_target(oa, ob),
         ))
 
     def got_zb(oa, ob):
-        arrived(cur.at[pl.ds(zb_at(oa, ob), 8)], zrecv.at[oa * 4 + ob])
+        arrived(cur.at[pl.ds(zb_at(oa, ob), 6)], zrecv.at[oa * 4 + ob])
 
     def send_own(lo, n, piece, origin=None):
         send_main(0, 0, lo, n, a_up, 1, 0, piece, origin)
@@ -123,10 +122,10 @@
 
     go(remote(
         cur_in.at[:, :, pl.ds(pl.multiple_of(oc * 128, 128), 128)],
-        cur.at[pl.ds((pb * 4 + pa) * 16 + 6, 6)], psend.at[0], precv.at[0], partner,
+        cur.at[pl.ds((pb * 4 + pa) * 18 + 6, 6)], psend.at[0], precv.at[0], partner,
     ))
     go(remote(
-        cur_in.at[pl.ds(0, 4), :, pl.ds(lane0, 128)], cur.at[pl.ds(own0 + 12, 4)],
+        own_half, cur.at[pl.ds(own0 + 12, 6)],
         zsend.at[16], zrecv.at[16], z_target(0, 0),
     ))
     send_own(0, 6, 0, own_half)
@@ -135,13 +134,13 @@
     arrived(cur.at[pl.ds(own0 + 6, 6)], precv.at[0])
     send_own(6, 6, 1)
     send_zb(0, 0)
-    arrived(cur.at[pl.ds(own0 + 12, 4)], zrecv.at[16])
-    send_own(12, 4, 2)
+    arrived(cur.at[pl.ds(own0 + 12, 6)], zrecv.at[16])
+    send_own(12, 6, 2)
     load("nb", nb_in, nb.at[pl.ds(0, 6)])
     go(remote(nb_in, nb.at[pl.ds(6, 6)], psend.at[2], precv.at[2], partner))
     cur[384] = jnp.zeros((128, 128), BF)
 
-    def slot_of(s):
+    def slot_of(s, field):
         halo = (s < 96) | (s >= 288)
         i = jnp.where(s < 96, s + 96, jnp.where(s >= 288, s - 288, s - 96))
         box_chip = lax.shift_right_arithmetic(i * 5462, 16)
@@ -152,9 +151,10 @@
         a = bx + c * (by - bx)
         b = by + c * (bx - by)
         b_hi = lax.shift_right_arithmetic(b, 1)
-        main = (a * 4 + b) * 16 + p
-        beyond = 256 + ((a * 2 + b - 2 * b_hi) * 2 + b_hi) * 8 + (p - 4)
-        slot = jnp.where(halo, jnp.where(p < 4, main + 12, beyond), main)
+        size, rim = (18, 6) if field else (16, 4)
+        main = (a * 4 + b) * size + p
+        beyond = 16 * size + ((a * 2 + b - 2 * b_hi) * 2 + b_hi) * (12 - rim) + (p - rim)
+        slot = jnp.where(halo, jnp.where(p < rim, main + 12, beyond), main)
         low = jnp.where(z == 0, 96, 0)
         high = jnp.where(z == 3, 288, 384)
         return jnp.where((s < low) | (s >= high), -1, slot)
@@ -167,7 +167,7 @@
         ref[128:256, :] = jnp.transpose(stage[:, 128:256])
 
     loads["src"].wait()
-    table(slot_of(sraw[0]).astype(F32), src)
+    table(slot_of(sraw[0], False).astype(F32), src)
     loads["tid"].wait()
     table(sraw[1].astype(F32), tid)
     loads["tt"].wait()
@@ -176,15 +176,12 @@
     tt_t[...] = jnp.transpose(wide[...]).astype(BF)
     loads["rad"].wait()
 
-    def pattern_block(at):
-        def pair(i, _):
-            two = jnp.concatenate([cur[at + 2 * i], cur[at + 2 * i + 1]], axis=1)
+    def pattern_block(at, box):
+        for i in range(8):
+            two = jnp.concatenate([cur[box(2 * i)], cur[box(2 * i + 1)]], axis=1)
             o = jnp.dot(rad[...], two, preferred_element_type=F32)
             bpat[2 * i] = o[:, :128].astype(BF)
             bpat[2 * i + 1] = o[:, 128:].astype(BF)
-            return 0
-
-        lax.fori_loop(0, 8, pair, 0)
 
         def turn(i, _):
             t0 = pl.multiple_of(i * 16, 16)
@@ -195,25 +192,36 @@
 
     def patterns(*blocks):
         for oa, ob in blocks:
-            pattern_block(base(oa, ob))
+            first = base(oa, ob)
+            at = (m4(pa - oa) * 4 + m4(pb - ob)) * 16
+            pattern_block(pl.multiple_of(at, 16), lambda i, first=first: first + i)
 
     def pattern_zb(oa, ob):
         got_zb(oa, ob)
         got_zb(oa, ob + 2)
-        g = m4(pa - oa) * 2 + lax.rem(m4(pb - ob), 2)
-        pattern_block(pl.multiple_of(256 + g * 16, 16))
+        a_, parity = m4(pa - oa), lax.rem(m4(pb - ob), 2)
+        g = a_ * 2 + parity
+        rim0 = (a_ * 4 + parity) * 18 + 16
+        over0 = 288 + g * 12
+
+        def box(i):
+            second, q = i // 8, i % 8
+            return rim0 + second * 36 + q if q < 2 else over0 + second * 6 + q - 2
+
+        pattern_block(pl.multiple_of(256 + g * 16, 16), box)
 
     n_iota = lax.broadcasted_iota(jnp.int32, (384, 128), 0).astype(F32)
     lane = lax.broadcasted_iota(jnp.int32, (TB, 128), 1)
 
     def box_row(jp):
-        group = lax.div(jp, 24)
-        rest = jp - group * 24
-        second = lax.div(rest, 12)
-        p = rest - second * 12
-        half = lax.div(group, 4)
-        a_ = group - 4 * half
-        b_ = m4(pb + jnp.where(half == 0, 2 - second, 3 - 3 * second))
+        late = jnp.where(jp >= 144, 1, 0)
+        at = jp - 144 * late
+        size = 36 - 24 * late
+        a_ = lax.div(at * (1 + 2 * late), 36)
+        rest = at - a_ * size
+        which = lax.div(rest, 12)
+        p = rest - which * 12
+        b_ = m4(pb + jnp.where(late == 1, 0, jnp.where(which == 2, 3, 2 - which)))
         chip_ = (b_ + c * (a_ - b_)) * 4 + a_ + c * (b_ - a_)
         return chip_ * 12 + lax.rem(p + 6 * c, 12)
 
@@ -240,7 +248,7 @@
                     bmat[h * 8 + 2 * it + p] = placed[h * TB : (h + 1) * TB].astype(BF)
             return 0
 
-        lax.fori_loop(0, 4, two_rows, 0)
+        lax.fori_loop(0, 4, two_rows, 0, unroll=4)
         j0 = pl.multiple_of(g * 16, 16)
 
         def turn(i, _):
@@ -256,95 +264,105 @@
         lax.fori_loop(lo, hi, lambda g, _: (mat_group(g), 0)[1], 0)
 
     def line_event(oa):
-        send_main(oa, 0, 0, 16, b_up, oa, 1, 0)
-        send_main(oa, 0, 0, 16, b_dn, oa, 3, 0)
+        send_main(oa, 0, 0, 18, b_up, oa, 1, 0)
+        send_main(oa, 0, 0, 18, b_dn, oa, 3, 0)
+
+    odd = lax.rem(y, 2)
+    line1 = 3 - 2 * c * (1 - odd)
+    line2 = 1 + c
+    line3 = 2 + c * (1 - 2 * odd)
+
+    def halves(oa, ob):
+        got_main(oa, ob, 0, 9, 0)
+        got_main(oa, ob, 9, 9, 1)
+        send_zb(oa, ob)
+
+    def ring_event(oa):
+        for ob, lo, to, piece in ((1, 0, b_up, 0), (3, 9, b_dn, 1)):
+            got_main(oa, ob, 0, 18, 0)
+            send_main(oa, ob, lo, 9, to, oa, 2, piece)
+            send_zb(oa, ob)
 
     for oa, ob in ((1, 0), (3, 0), (0, 1), (0, 3)):
         got_main(oa, ob, 0, 6, 0)
         got_main(oa, ob, 6, 6, 1)
         if (oa, ob) == (1, 0):
-            send_main(1, 0, 0, 8, a_up, 2, 0, 0)
+            send_main(1, 0, 0, 9, a_up, 2, 0, 0)
         if (oa, ob) == (0, 1):
-            send_main(0, 1, 0, 8, b_up, 0, 2, 0)
+            send_main(0, 1, 0, 9, b_up, 0, 2, 0)
         send_zb(oa, ob)
-    got_main(3, 0, 12, 4, 2)
-    send_main(3, 0, 8, 8, a_dn, 2, 0, 1)
-    line_event(3)
-    got_main(1, 0, 12, 4, 2)
-    line_event(1)
-    got_main(0, 3, 12, 4, 2)
-    send_main(0, 3, 8, 8, b_dn, 0, 2, 1)
-    got_main(0, 1, 12, 4, 2)
+    got_main(3, 0, 12, 6, 2)
+    send_main(3, 0, 9, 9, a_dn, 2, 0, 1)
+    got_main(1, 0, 12, 6, 2)
+    line_event(line1)
+    got_main(0, 3, 12, 6, 2)
+    send_main(0, 3, 9, 9, b_dn, 0, 2, 1)
+    got_main(0, 1, 12, 6, 2)
     mats(0, 1)
     patterns((0, 0))
-
-    def halves(oa, ob):
-        got_main(oa, ob, 0, 8, 0)
-        got_main(oa, ob, 8, 8, 1)
-        send_zb(oa, ob)
-
-    def ring_event(oa):
-        for ob, lo, to, piece in ((1, 0, b_up, 0), (3, 8, b_dn, 1)):
-            got_main(oa, ob, 0, 16, 0)
-            send_main(oa, ob, lo, 8, to, oa, 2, piece)
-            send_zb(oa, ob)
-
     halves(2, 0)
-    line_event(2)
+    line_event(line2)
+    line_event(line3)
     mats(1, 2)
     patterns((1, 0))
-    ring_event(3)
+    ring_event(line1)
     mats(2, 3)
     patterns((3, 0), (2, 0))
-    ring_event(1)
     halves(0, 2)
     mats(3, 5)
     patterns((0, 1), (0, 3))
-    ring_event(2)
+    ring_event(line2)
     mats(5, 7)
-    patterns((3, 1), (3, 3), (0, 2))
-    halves(3, 2)
+    patterns((line1, 1), (line1, 3), (0, 2))
+    halves(line1, 2)
     mats(7, 9)
-    patterns((1, 1), (1, 3))
-    halves(1, 2)
+    patterns((line2, 1), (line2, 3))
+    ring_event(line3)
     mats(9, 12)
-    patterns((2, 1), (2, 3), (3, 2), (1, 2))
-    halves(2, 2)
-    patterns((2, 2))
-    for oa, ob in ((0, 0), (0, 1), (3, 1), (1, 1), (3, 0), (1, 0), (2, 1), (2, 0)):
+    halves(line2, 2)
+    patterns((line3, 1), (line3, 3), (line1, 2), (line2, 2))
+    halves(line3, 2)
+    patterns((line3, 2))
+    for oa, ob in (
+        (0, 0), (0, 1), (line1, 1), (line1, 0), (line2, 1), (line2, 0), (line3, 1), (line3, 0)
+    ):
         pattern_zb(oa, ob)
 
+    first_row, rows_of = (0, 144), (36, 12)
     own_copies = []
 
     def chunk(h, k):
         n = h * 3 + k
-        j0 = h * 96
+        j0, n_rows = first_row[h], rows_of[h]
+        n_half, n_tiles = n_rows // 2, n_rows // 4
 
         def one(i, _):
             t = k * TCH + i
-            btr[i] = jnp.dot(mat[t, j0 : j0 + 96, :], pat[t], preferred_element_type=F32).astype(BF)
-            return 0
-
-        lax.fori_loop(0, TCH, one, 0, unroll=2)
+            o = jnp.dot(mat[t, j0 : j0 + 4 * n_rows, :], pat[t], preferred_element_type=F32)
+            btr[i, 0 : 4 * n_rows] = o.astype(BF)
+            return 0
+
+        lax.fori_loop(0, TCH, one, 0, unroll=8)
 
         def pack(i, _):
-            r0 = pl.multiple_of(lax.rem(i, 6) * 16, 16)
-            t0 = pl.multiple_of(lax.div(i, 6) * 16, 16)
+            r0 = pl.multiple_of(lax.rem(i, n_tiles) * 16, 16)
+            t0 = pl.multiple_of(lax.div(i, n_tiles) * 16, 16)
             tx[pl.ds(j0 + r0, 16), pl.ds(k * TCH + t0, 16), :] = jnp.swapaxes(
                 btr[pl.ds(t0, 16), pl.ds(r0, 16), :], 0, 1
             )
             return 0
 
-        lax.fori_loop(0, 12, pack, 0, unroll=2)
+        lax.fori_loop(0, 2 * n_tiles, pack, 0, unroll=2)
         ts = pl.ds(k * TCH, TCH)
-        here = pl.ds(h * 24, 24)
+        here = pl.ds(h * 36, n_rows)
         there = rx_at(pa, k)
-        far = j0 + m4(pa + 2) * 24
-        go(remote(tx.at[pl.ds(far, 12), ts], relay.at[0, n], rsend.at[n * 6 + 2], rrecv.at[n * 6 + 2], a_up))
-        go(remote(tx.at[pl.ds(far + 12, 12), ts], relay.at[1, n], rsend.at[n * 6 + 3], rrecv.at[n * 6 + 3], a_dn))
-        go(remote(tx.at[pl.ds(j0 + m4(pa + 1) * 24, 24), ts], rx.at[here, there], rsend.at[n * 6], rrecv.at[n * 6], a_up))
-        go(remote(tx.at[pl.ds(j0 + m4(pa - 1) * 24, 24), ts], rx.at[here, there], rsend.at[n * 6 + 1], rrecv.at[n * 6 + 1], a_dn))
-        own = pltpu.make_async_copy(tx.at[pl.ds(j0 + pa * 24, 24), ts], rx.at[here, there], lsem.at[10 + n])
+        far = j0 + m4(pa + 2) * n_rows
+        hop_rows = pl.ds(0, n_half)
+        go(remote(tx.at[pl.ds(far, n_half), ts], relay.at[0, n, hop_rows], rsend.at[n * 6 + 2], rrecv.at[n * 6 + 2], a_up))
+        go(remote(tx.at[pl.ds(far + n_half, n_half), ts], relay.at[1, n, hop_rows], rsend.at[n * 6 + 3], rrecv.at[n * 6 + 3], a_dn))
+        go(remote(tx.at[pl.ds(j0 + m4(pa + 1) * n_rows, n_rows), ts], rx.at[here, there], rsend.at[n * 6], rrecv.at[n * 6], a_up))
+        go(remote(tx.at[pl.ds(j0 + m4(pa - 1) * n_rows, n_rows), ts], rx.at[here, there], rsend.at[n * 6 + 1], rrecv.at[n * 6 + 1], a_dn))
+        own = pltpu.make_async_copy(tx.at[pl.ds(j0 + pa * n_rows, n_rows), ts], rx.at[here, there], lsem.at[10 + n])
         own.start()
         own_copies.append(own)
 
@@ -353,22 +371,24 @@
 
     def forward(h, k):
         n = h * 3 + k
-        arrived(relay.at[0, n], rrecv.at[n * 6 + 2])
-        go(remote(relay.at[0, n], rx.at[pl.ds(h * 24, 12), rx_at(m4(pa - 1), k)],
-                  rsend.at[n * 6 + 4], rrecv.at[n * 6 + 4], a_up))
-        arrived(relay.at[1, n], rrecv.at[n * 6 + 3])
-        go(remote(relay.at[1, n], rx.at[pl.ds(h * 24 + 12, 12), rx_at(m4(pa + 1), k)],
-                  rsend.at[n * 6 + 5], rrecv.at[n * 6 + 5], a_dn))
+        n_half = rows_of[h] // 2
+        for way, o, to in ((0, -1, a_up), (1, 1, a_dn)):
+            held = relay.at[way, n, pl.ds(0, n_half)]
+            arrived(held, rrecv.at[n * 6 + 2 + way])
+            go(remote(held, rx.at[pl.ds(h * 36 + way * n_half, n_half), rx_at(m4(pa + o), k)],
+                      rsend.at[n * 6 + 4 + way], rrecv.at[n * 6 + 4 + way], to))
 
     def all_here(h):
-        here = pl.ds(h * 24, 24)
+        n_half = rows_of[h] // 2
+        here = pl.ds(h * 36, 2 * n_half)
         for k in range(3):
             n = h * 3 + k
             own_copies[n].wait()
             arrived(rx.at[here, rx_at(m4(pa - 1), k)], rrecv.at[n * 6])
             arrived(rx.at[here, rx_at(m4(pa + 1), k)], rrecv.at[n * 6 + 1])
-            arrived(rx.at[pl.ds(h * 24, 12), rx_at(m4(pa + 2), k)], rrecv.at[n * 6 + 4])
-            arrived(rx.at[pl.ds(h * 24 + 12, 12), rx_at(m4(pa + 2), k)], rrecv.at[n * 6 + 5])
+            for way in range(2):
+                arrived(rx.at[pl.ds(h * 36 + way * n_half, n_half), rx_at(m4(pa + 2), k)],
+                        rrecv.at[n * 6 + 4 + way])
 
     def near_boxes(which, lo, hi):
         def box(i, _):
@@ -409,8 +429,6 @@
     chunk(0, 1)
     forward(0, 0)
     chunk(0, 2)
-    forward(0, 1)
-    chunk(1, 0)
     loads["rcv"].wait()
     loads["offs"].wait()
     k_at = lax.broadcasted_iota(jnp.int32, (8, 384), 1) + pb * 384
@@ -423,30 +441,43 @@
     loads["near"].wait()
     arrived(near_v.at[1], precv.at[1])
     near_s = near_v[...]
-    near_s = slot_of(jnp.where(near_s < 0, -1, near_s + 48))
+    near_s = slot_of(jnp.where(near_s < 0, -1, near_s + 48), True)
     near_m[...] = jnp.where(near_s < 0, 384, near_s)
+    forward(0, 1)
+    load("ns", near_m, ns)
+    chunk(1, 0)
+    chunk(1, 1)
     forward(0, 2)
-    load("ns", near_m, ns)
-    chunk(1, 1)
+    chunk(1, 2)
     loads["ns"].wait()
     loads["nb"].wait()
-    near_boxes(0, 0, 2)
+    near_boxes(0, 0, 4)
     forward(1, 0)
-    chunk(1, 2)
     all_here(0)
-    partial_to(0, 2, b_far)
+
+    def put_far(w, v):
+        ps[1, w] = v.astype(BF)
+
+    contract(0, put_far)
+    go(remote(ps.at[1, pl.ds(0, 6)], hop.at[0], ssend.at[1], srecv.at[1], b_up))
+    go(remote(ps.at[1, pl.ds(6, 6)], hop.at[1], ssend.at[3], srecv.at[3], b_dn))
     partial_to(1, 1, b_up)
+    partial_to(2, 3, b_dn)
     forward(1, 1)
-    near_boxes(0, 2, 5)
+    arrived(hop.at[0], srecv.at[1])
+    go(remote(hop.at[0], pr.at[1, pl.ds(0, 6)], ssend.at[4], srecv.at[4], b_up))
+    arrived(hop.at[1], srecv.at[3])
+    go(remote(hop.at[1], pr.at[1, pl.ds(6, 6)], ssend.at[5], srecv.at[5], b_dn))
     forward(1, 2)
-    near_boxes(0, 5, 6)
+    near_boxes(0, 4, 6)
     arrived(nb.at[pl.ds(6, 6)], precv.at[2])
     near_boxes(1, 0, 6)
     all_here(1)
-    partial_to(2, 3, b_dn)
     contract(3, put_acc)
-    for o in (2, 1, 3):
-        arrived(pr.at[o - 1], srecv.at[o - 1])
+    arrived(pr.at[0], srecv.at[0])
+    arrived(pr.at[2], srecv.at[2])
+    arrived(pr.at[1, pl.ds(0, 6)], srecv.at[4])
+    arrived(pr.at[1, pl.ds(6, 6)], srecv.at[5])
 
     def finish(which):
         def one(i, _):
@@ -485,13 +516,14 @@
             pltpu.VMEM((TB, 384, 128), BF),
             pltpu.VMEM((192, TB, 128), BF),
             pltpu.VMEM((48, 4 * TB, 128), BF),
-            pltpu.VMEM((2, NCH, 12, TCH, 128), BF),
+            pltpu.VMEM((2, NCH, 18, TCH, 128), BF),
+            pltpu.VMEM((2, 6, 128, 128), BF),
             pltpu.VMEM((3, 12, 128, 128), BF),
             pltpu.VMEM((3, 12, 128, 128), BF),
             pltpu.VMEM((12, 128, 128), F32),
             pltpu.VMEM((16, TB, 128), BF),
             pltpu.VMEM((16, TB, 384), BF),
-            pltpu.VMEM((TCH, 96, 128), BF),
+            pltpu.VMEM((TCH, 144, 128), BF),
             pltpu.VMEM((TB, 128), BF),
             pltpu.VMEM((128, 384), BF),
             pltpu.VMEM((128, 384), BF),
@@ -516,8 +548,8 @@
             dma((17,)),
             dma((36,)),
             dma((36,)),
-            dma((3,)),
-            dma((3,)),
+            dma((6,)),
+            dma((6,)),
         ],
         compiler_params=pltpu.CompilerParams(
             collective_id=0, has_side_effects=True, vmem_limit_bytes=67043328

time: 139 us -> 116 us (0.83)
  Pallas kernels: 137 us -> 114 us
    pallas_call x1, Pallas kernels: 137 us -> 114 us  [shards(): pl.pallas_call(body, out_shape=jax.ShapeDtypeStruct((6, 128, 256), BF), i...]
where the time goes in v3:
time: 116 us
  Pallas kernels  114 us (98%)
  local copies, waits for them, and re-layouts  1.77 us (2%)
    pallas_call x1, Pallas kernels, shards(): pl.pallas_call(body, out_shape=jax.ShapeDtypeStruct((6, 128, 256), BF), i...  114 us

profile of v3, /device:TPU:1, one launch (start us, length us, event | category | flops | bytes accessed | tf_op | source)
XLA Modules:
  0.0 115.8 jit_solution(2240032663219102764)
XLA Ops:
  0.0 114.0 %fmm.1 = bf16[6,128,256]{2,1,0:T(8,128)(2,1)} custom-call(bf16[6,128,256]{2,1,0:T(8,128)(2,1)} %bitcast.12, bf16[1536,128]{1,0:T(8,128)(2,1)} %rad_in.1, bf16[128,1536]{1,0:T(8,128)(2,1)} %rcv_in.1, bf16[6,27,128,128]{3,2,1,0:T(8,128)(2,1)} %bitcast.10, s32[6,1,27]{2,1,0:T(1,128)} %bitcast.15, bf16[316,1536]{1,0:T(8,128)(2,1)} %tt_in.1, s32[48,192]{1,0:T(8,128)} %bitcast.13, ...), custom_call_target="tpu_custom_call" | custom-call | tf_op jit(solution)/shard_map/fmm/pallas_call | solution.py:507
  114.0 1.8 %copy.11 = bf16[1,6,128,256]{3,2,1,0:T(8,128)(2,1)} copy(bf16[1,6,128,256]{3,2,1,0:T(8,128)(2,1)} %bitcast.11) | data formatting | bytes 786432

commit v4 on v3

--- a/solution.py
+++ b/solution.py
@@ -11,6 +11,9 @@
 TB = 96
 NCH = 6
 TCH = TB // 3
+RIM = 6
+BLK = 12 + RIM
+HALF = (BLK + 1) // 2
 
 
 def m4(v):
@@ -51,7 +54,7 @@
     own_half = cur_in.at[:, :, pl.ds(lane0, 128)]
 
     def base(oa, ob):
-        return (m4(pa - oa) * 4 + m4(pb - ob)) * 18
+        return (m4(pa - oa) * 4 + m4(pb - ob)) * BLK
 
     own0 = base(0, 0)
     loads = {}
@@ -103,16 +106,16 @@
 
     def zb_at(oa, ob):
         a_, b_ = m4(pa - oa), m4(pb - ob)
-        return 288 + ((a_ * 2 + lax.rem(b_, 2)) * 2 + lax.div(b_, 2)) * 6
+        return 16 * BLK + ((a_ * 2 + lax.rem(b_, 2)) * 2 + lax.div(b_, 2)) * (12 - RIM)
 
     def send_zb(oa, ob):
         go(remote(
-            cur.at[pl.ds(base(oa, ob) + 6, 6)], cur.at[pl.ds(zb_at(oa, ob), 6)],
+            cur.at[pl.ds(base(oa, ob) + RIM, 12 - RIM)], cur.at[pl.ds(zb_at(oa, ob), 12 - RIM)],
             zsend.at[oa * 4 + ob], zrecv.at[oa * 4 + ob], z_target(oa, ob),
         ))
 
     def got_zb(oa, ob):
-        arrived(cur.at[pl.ds(zb_at(oa, ob), 6)], zrecv.at[oa * 4 + ob])
+        arrived(cur.at[pl.ds(zb_at(oa, ob), 12 - RIM)], zrecv.at[oa * 4 + ob])
 
     def send_own(lo, n, piece, origin=None):
         send_main(0, 0, lo, n, a_up, 1, 0, piece, origin)
@@ -122,10 +125,10 @@
 
     go(remote(
         cur_in.at[:, :, pl.ds(pl.multiple_of(oc * 128, 128), 128)],
-        cur.at[pl.ds((pb * 4 + pa) * 18 + 6, 6)], psend.at[0], precv.at[0], partner,
+        cur.at[pl.ds((pb * 4 + pa) * BLK + 6, 6)], psend.at[0], precv.at[0], partner,
     ))
     go(remote(
-        own_half, cur.at[pl.ds(own0 + 12, 6)],
+        cur_in.at[pl.ds(0, RIM), :, pl.ds(lane0, 128)], cur.at[pl.ds(own0 + 12, RIM)],
         zsend.at[16], zrecv.at[16], z_target(0, 0),
     ))
     send_own(0, 6, 0, own_half)
@@ -134,8 +137,8 @@
     arrived(cur.at[pl.ds(own0 + 6, 6)], precv.at[0])
     send_own(6, 6, 1)
     send_zb(0, 0)
-    arrived(cur.at[pl.ds(own0 + 12, 6)], zrecv.at[16])
-    send_own(12, 6, 2)
+    arrived(cur.at[pl.ds(own0 + 12, RIM)], zrecv.at[16])
+    send_own(12, RIM, 2)
     load("nb", nb_in, nb.at[pl.ds(0, 6)])
     go(remote(nb_in, nb.at[pl.ds(6, 6)], psend.at[2], precv.at[2], partner))
     cur[384] = jnp.zeros((128, 128), BF)
@@ -151,7 +154,7 @@
         a = bx + c * (by - bx)
         b = by + c * (bx - by)
         b_hi = lax.shift_right_arithmetic(b, 1)
-        size, rim = (18, 6) if field else (16, 4)
+        size, rim = (BLK, RIM) if field else (16, 4)
         main = (a * 4 + b) * size + p
         beyond = 16 * size + ((a * 2 + b - 2 * b_hi) * 2 + b_hi) * (12 - rim) + (p - rim)
         slot = jnp.where(halo, jnp.where(p < rim, main + 12, beyond), main)
@@ -201,12 +204,12 @@
         got_zb(oa, ob + 2)
         a_, parity = m4(pa - oa), lax.rem(m4(pb - ob), 2)
         g = a_ * 2 + parity
-        rim0 = (a_ * 4 + parity) * 18 + 16
-        over0 = 288 + g * 12
+        rim0 = (a_ * 4 + parity) * BLK + 16
+        over0 = 16 * BLK + g * 2 * (12 - RIM)
 
         def box(i):
             second, q = i // 8, i % 8
-            return rim0 + second * 36 + q if q < 2 else over0 + second * 6 + q - 2
+            return rim0 + second * 2 * BLK + q if q < RIM - 4 else over0 + second * (12 - RIM) + q - (RIM - 4)
 
         pattern_block(pl.multiple_of(256 + g * 16, 16), box)
 
@@ -264,8 +267,8 @@
         lax.fori_loop(lo, hi, lambda g, _: (mat_group(g), 0)[1], 0)
 
     def line_event(oa):
-        send_main(oa, 0, 0, 18, b_up, oa, 1, 0)
-        send_main(oa, 0, 0, 18, b_dn, oa, 3, 0)
+        send_main(oa, 0, 0, BLK, b_up, oa, 1, 0)
+        send_main(oa, 0, 0, BLK, b_dn, oa, 3, 0)
 
     odd = lax.rem(y, 2)
     line1 = 3 - 2 * c * (1 - odd)
@@ -273,39 +276,39 @@
     line3 = 2 + c * (1 - 2 * odd)
 
     def halves(oa, ob):
-        got_main(oa, ob, 0, 9, 0)
-        got_main(oa, ob, 9, 9, 1)
+        got_main(oa, ob, 0, HALF, 0)
+        got_main(oa, ob, HALF, BLK - HALF, 1)
         send_zb(oa, ob)
 
     def ring_event(oa):
-        for ob, lo, to, piece in ((1, 0, b_up, 0), (3, 9, b_dn, 1)):
-            got_main(oa, ob, 0, 18, 0)
-            send_main(oa, ob, lo, 9, to, oa, 2, piece)
+        for ob, lo, n, to, piece in ((1, 0, HALF, b_up, 0), (3, HALF, BLK - HALF, b_dn, 1)):
+            got_main(oa, ob, 0, BLK, 0)
+            send_main(oa, ob, lo, n, to, oa, 2, piece)
             send_zb(oa, ob)
 
     for oa, ob in ((1, 0), (3, 0), (0, 1), (0, 3)):
         got_main(oa, ob, 0, 6, 0)
         got_main(oa, ob, 6, 6, 1)
         if (oa, ob) == (1, 0):
-            send_main(1, 0, 0, 9, a_up, 2, 0, 0)
+            send_main(1, 0, 0, HALF, a_up, 2, 0, 0)
         if (oa, ob) == (0, 1):
-            send_main(0, 1, 0, 9, b_up, 0, 2, 0)
+            send_main(0, 1, 0, HALF, b_up, 0, 2, 0)
         send_zb(oa, ob)
-    got_main(3, 0, 12, 6, 2)
-    send_main(3, 0, 9, 9, a_dn, 2, 0, 1)
-    got_main(1, 0, 12, 6, 2)
+    got_main(3, 0, 12, RIM, 2)
+    send_main(3, 0, HALF, BLK - HALF, a_dn, 2, 0, 1)
+    got_main(1, 0, 12, RIM, 2)
     line_event(line1)
-    got_main(0, 3, 12, 6, 2)
-    send_main(0, 3, 9, 9, b_dn, 0, 2, 1)
-    got_main(0, 1, 12, 6, 2)
+    got_main(0, 3, 12, RIM, 2)
+    send_main(0, 3, HALF, BLK - HALF, b_dn, 0, 2, 1)
+    got_main(0, 1, 12, RIM, 2)
     mats(0, 1)
     patterns((0, 0))
     halves(2, 0)
     line_event(line2)
-    line_event(line3)
     mats(1, 2)
     patterns((1, 0))
     ring_event(line1)
+    line_event(line3)
     mats(2, 3)
     patterns((3, 0), (2, 0))
     halves(0, 2)

time: 116 us -> 112 us (0.966)
  Pallas kernels: 114 us -> 110 us
    pallas_call x1, Pallas kernels: 114 us -> 110 us  [shards(): pl.pallas_call(body, out_shape=jax.ShapeDtypeStruct((6, 128, 256), BF), i...]
where the time goes in v4:
time: 112 us
  Pallas kernels  110 us (98%)
  local copies, waits for them, and re-layouts  1.77 us (2%)
    pallas_call x1, Pallas kernels, shards(): pl.pallas_call(body, out_shape=jax.ShapeDtypeStruct((6, 128, 256), BF), i...  110 us

profile of v4, /device:TPU:1, one launch (start us, length us, event | category | flops | bytes accessed | tf_op | source)
XLA Modules:
  0.0 111.7 jit_solution(630602423998637453)
XLA Ops:
  0.0 109.9 %fmm.1 = bf16[6,128,256]{2,1,0:T(8,128)(2,1)} custom-call(bf16[6,128,256]{2,1,0:T(8,128)(2,1)} %bitcast.12, bf16[1536,128]{1,0:T(8,128)(2,1)} %rad_in.1, bf16[128,1536]{1,0:T(8,128)(2,1)} %rcv_in.1, bf16[6,27,128,128]{3,2,1,0:T(8,128)(2,1)} %bitcast.10, s32[6,1,27]{2,1,0:T(1,128)} %bitcast.15, bf16[316,1536]{1,0:T(8,128)(2,1)} %tt_in.1, s32[48,192]{1,0:T(8,128)} %bitcast.13, ...), custom_call_target="tpu_custom_call" | custom-call | tf_op jit(solution)/shard_map/fmm/pallas_call | solution.py:510
  109.9 1.8 %copy.11 = bf16[1,6,128,256]{3,2,1,0:T(8,128)(2,1)} copy(bf16[1,6,128,256]{3,2,1,0:T(8,128)(2,1)} %bitcast.11) | data formatting | bytes 786432

commit v5 on v4

--- a/solution.py
+++ b/solution.py
@@ -9,8 +9,7 @@
 BF = jnp.bfloat16
 F32 = jnp.float32
 TB = 96
-NCH = 6
-TCH = TB // 3
+CHUNKS = ((0, 0, 16), (0, 16, 32), (0, 48, 32), (0, 80, 16), (1, 0, 32), (1, 32, 32), (1, 64, 32))
 RIM = 6
 BLK = 12 + RIM
 HALF = (BLK + 1) // 2
@@ -22,7 +21,7 @@
 
 def body(
     cur_in, rad_in, rcv_in, nb_in, near_in, tt_in, src_in, tid_in, offs_in, out,
-    cur, nb, mat, pat, tx, rx, relay, hop, ps, pr, acc, bpat, bmat, btr, rad, rcv, rw, fin,
+    cur, nb, mat, pat, tx, rx, relay, relay2, hop, ps, pr, acc, bpat, bmat, btr, rad, rcv, rw, fin,
     near_v, near_m, ns, tts, wide, tt_t, sraw, stage, src, tid, offs,
     lsem, psend, precv, asend, arecv, zsend, zrecv, rsend, rrecv, ssend, srecv,
 ):
@@ -334,63 +333,69 @@
     first_row, rows_of = (0, 144), (36, 12)
     own_copies = []
 
-    def chunk(h, k):
-        n = h * 3 + k
+    def chunk(n):
+        h, t_first, n_dirs = CHUNKS[n]
         j0, n_rows = first_row[h], rows_of[h]
         n_half, n_tiles = n_rows // 2, n_rows // 4
 
         def one(i, _):
-            t = k * TCH + i
+            t = t_first + i
             o = jnp.dot(mat[t, j0 : j0 + 4 * n_rows, :], pat[t], preferred_element_type=F32)
             btr[i, 0 : 4 * n_rows] = o.astype(BF)
             return 0
 
-        lax.fori_loop(0, TCH, one, 0, unroll=8)
+        lax.fori_loop(0, n_dirs, one, 0, unroll=8)
 
         def pack(i, _):
             r0 = pl.multiple_of(lax.rem(i, n_tiles) * 16, 16)
             t0 = pl.multiple_of(lax.div(i, n_tiles) * 16, 16)
-            tx[pl.ds(j0 + r0, 16), pl.ds(k * TCH + t0, 16), :] = jnp.swapaxes(
+            tx[pl.ds(j0 + r0, 16), pl.ds(t_first + t0, 16), :] = jnp.swapaxes(
                 btr[pl.ds(t0, 16), pl.ds(r0, 16), :], 0, 1
             )
             return 0
 
-        lax.fori_loop(0, 2 * n_tiles, pack, 0, unroll=2)
-        ts = pl.ds(k * TCH, TCH)
+        lax.fori_loop(0, n_tiles * n_dirs // 16, pack, 0, unroll=3)
+        ts = pl.ds(t_first, n_dirs)
         here = pl.ds(h * 36, n_rows)
-        there = rx_at(pa, k)
+        there = rx_at(pa, n)
         far = j0 + m4(pa + 2) * n_rows
-        hop_rows = pl.ds(0, n_half)
-        go(remote(tx.at[pl.ds(far, n_half), ts], relay.at[0, n, hop_rows], rsend.at[n * 6 + 2], rrecv.at[n * 6 + 2], a_up))
-        go(remote(tx.at[pl.ds(far + n_half, n_half), ts], relay.at[1, n, hop_rows], rsend.at[n * 6 + 3], rrecv.at[n * 6 + 3], a_dn))
-        go(remote(tx.at[pl.ds(j0 + m4(pa + 1) * n_rows, n_rows), ts], rx.at[here, there], rsend.at[n * 6], rrecv.at[n * 6], a_up))
-        go(remote(tx.at[pl.ds(j0 + m4(pa - 1) * n_rows, n_rows), ts], rx.at[here, there], rsend.at[n * 6 + 1], rrecv.at[n * 6 + 1], a_dn))
+        for way, to in ((0, a_up), (1, a_dn)):
+            go(remote(tx.at[pl.ds(far + way * n_half, n_half), ts], held(way, n),
+                      rsend.at[n * 6 + 2 + way], rrecv.at[n * 6 + 2 + way], to))
+        for way, o, to in ((0, 1, a_up), (1, -1, a_dn)):
+            go(remote(tx.at[pl.ds(j0 + m4(pa + o) * n_rows, n_rows), ts], rx.at[here, there],
+                      rsend.at[n * 6 + way], rrecv.at[n * 6 + way], to))
         own = pltpu.make_async_copy(tx.at[pl.ds(j0 + pa * n_rows, n_rows), ts], rx.at[here, there], lsem.at[10 + n])
         own.start()
         own_copies.append(own)
 
-    def rx_at(a_, k):
-        return pl.ds(pl.multiple_of(a_ * TB + k * TCH, TCH), TCH)
-
-    def forward(h, k):
-        n = h * 3 + k
+    def rx_at(a_, n):
+        _, t_first, n_dirs = CHUNKS[n]
+        return pl.ds(pl.multiple_of(a_ * TB + t_first, 16), n_dirs)
+
+    def held(way, n):
+        h, _, n_dirs = CHUNKS[n]
+        return relay.at[way, n, :, pl.ds(0, n_dirs)] if h == 0 else relay2.at[way, n - 4]
+
+    def forward(n):
+        h = CHUNKS[n][0]
         n_half = rows_of[h] // 2
         for way, o, to in ((0, -1, a_up), (1, 1, a_dn)):
-            held = relay.at[way, n, pl.ds(0, n_half)]
-            arrived(held, rrecv.at[n * 6 + 2 + way])
-            go(remote(held, rx.at[pl.ds(h * 36 + way * n_half, n_half), rx_at(m4(pa + o), k)],
+            arrived(held(way, n), rrecv.at[n * 6 + 2 + way])
+            go(remote(held(way, n), rx.at[pl.ds(h * 36 + way * n_half, n_half), rx_at(m4(pa + o), n)],
                       rsend.at[n * 6 + 4 + way], rrecv.at[n * 6 + 4 + way], to))
 
     def all_here(h):
         n_half = rows_of[h] // 2
         here = pl.ds(h * 36, 2 * n_half)
-        for k in range(3):
-            n = h * 3 + k
+        for n in range(len(CHUNKS)):
+            if CHUNKS[n][0] != h:
+                continue
             own_copies[n].wait()
-            arrived(rx.at[here, rx_at(m4(pa - 1), k)], rrecv.at[n * 6])
-            arrived(rx.at[here, rx_at(m4(pa + 1), k)], rrecv.at[n * 6 + 1])
+            arrived(rx.at[here, rx_at(m4(pa - 1), n)], rrecv.at[n * 6])
+            arrived(rx.at[here, rx_at(m4(pa + 1), n)], rrecv.at[n * 6 + 1])
             for way in range(2):
-                arrived(rx.at[pl.ds(h * 36 + way * n_half, n_half), rx_at(m4(pa + 2), k)],
+                arrived(rx.at[pl.ds(h * 36 + way * n_half, n_half), rx_at(m4(pa + 2), n)],
                         rrecv.at[n * 6 + 4 + way])
 
     def near_boxes(which, lo, hi):
@@ -418,20 +423,13 @@
 
         lax.fori_loop(0, 6, pair, 0)
 
-    def partial_to(group, o, to):
-        def put(w, v):
-            ps[o - 1, w] = v.astype(BF)
-
-        contract(group, put)
-        go(remote(ps.at[o - 1], pr.at[o - 1], ssend.at[o - 1], srecv.at[o - 1], to))
-
     def put_acc(w, v):
         acc[w] = acc[w] + v
 
-    chunk(0, 0)
-    chunk(0, 1)
-    forward(0, 0)
-    chunk(0, 2)
+    chunk(0)
+    chunk(1)
+    forward(0)
+    chunk(2)
     loads["rcv"].wait()
     loads["offs"].wait()
     k_at = lax.broadcasted_iota(jnp.int32, (8, 384), 1) + pb * 384
@@ -446,46 +444,61 @@
     near_s = near_v[...]
     near_s = slot_of(jnp.where(near_s < 0, -1, near_s + 48), True)
     near_m[...] = jnp.where(near_s < 0, 384, near_s)
-    forward(0, 1)
+    forward(1)
     load("ns", near_m, ns)
-    chunk(1, 0)
-    chunk(1, 1)
-    forward(0, 2)
-    chunk(1, 2)
+    chunk(3)
+    chunk(4)
+    forward(2)
+    chunk(5)
+    chunk(6)
     loads["ns"].wait()
     loads["nb"].wait()
-    near_boxes(0, 0, 4)
-    forward(1, 0)
+    near_boxes(0, 0, 1)
+    forward(3)
+    near_boxes(0, 1, 4)
+    forward(4)
     all_here(0)
 
-    def put_far(w, v):
-        ps[1, w] = v.astype(BF)
-
-    contract(0, put_far)
-    go(remote(ps.at[1, pl.ds(0, 6)], hop.at[0], ssend.at[1], srecv.at[1], b_up))
-    go(remote(ps.at[1, pl.ds(6, 6)], hop.at[1], ssend.at[3], srecv.at[3], b_dn))
-    partial_to(1, 1, b_up)
-    partial_to(2, 3, b_dn)
-    forward(1, 1)
-    arrived(hop.at[0], srecv.at[1])
-    go(remote(hop.at[0], pr.at[1, pl.ds(0, 6)], ssend.at[4], srecv.at[4], b_up))
-    arrived(hop.at[1], srecv.at[3])
-    go(remote(hop.at[1], pr.at[1, pl.ds(6, 6)], ssend.at[5], srecv.at[5], b_dn))
-    forward(1, 2)
+    def put_ps(slot):
+        def put(w, v):
+            ps[slot, w] = v.astype(BF)
+
+        return put
+
+    contract(0, put_ps(2))
+    go(remote(ps.at[2, pl.ds(0, 6)], hop.at[0], ssend.at[0], srecv.at[0], b_up))
+    go(remote(ps.at[2, pl.ds(6, 6)], hop.at[1], ssend.at[1], srecv.at[1], b_dn))
+    contract(1, put_ps(0))
+    go(remote(ps.at[0, pl.ds(6, 6)], pr.at[0, pl.ds(6, 6)], ssend.at[2], srecv.at[2], b_up))
+    contract(2, put_ps(1))
+    go(remote(ps.at[1, pl.ds(0, 6)], pr.at[1, pl.ds(0, 6)], ssend.at[3], srecv.at[3], b_dn))
+    forward(5)
+    forward(6)
     near_boxes(0, 4, 6)
+    for way, to in ((0, b_up), (1, b_dn)):
+        arrived(hop.at[way], srecv.at[way])
+
+        def join(i, _, way=way):
+            w = way * 6 + i
+            ps[way, w] = (ps[way, w].astype(F32) + hop[way, i].astype(F32)).astype(BF)
+            return 0
+
+        lax.fori_loop(0, 6, join, 0)
+        part = pl.ds(way * 6, 6)
+        go(remote(ps.at[way, part], pr.at[way, part], ssend.at[4 + way], srecv.at[4 + way], to))
     arrived(nb.at[pl.ds(6, 6)], precv.at[2])
     near_boxes(1, 0, 6)
     all_here(1)
     contract(3, put_acc)
-    arrived(pr.at[0], srecv.at[0])
-    arrived(pr.at[2], srecv.at[2])
-    arrived(pr.at[1, pl.ds(0, 6)], srecv.at[4])
+    arrived(pr.at[0, pl.ds(6, 6)], srecv.at[2])
+    arrived(pr.at[1, pl.ds(0, 6)], srecv.at[3])
+    arrived(pr.at[0, pl.ds(0, 6)], srecv.at[4])
     arrived(pr.at[1, pl.ds(6, 6)], srecv.at[5])
 
     def finish(which):
         def one(i, _):
             w = which * 6 + i
-            total = acc[w] + pr[0, w].astype(F32) + pr[1, w].astype(F32) + pr[2, w].astype(F32)
+            total = acc[w] + pr[0, w].astype(F32) + pr[1, w].astype(F32)
             fin[which, i] = total.astype(BF)
             return 0
 
@@ -496,7 +509,7 @@
     finish(1)
     go(remote(fin.at[1], out.at[:, :, mine], psend.at[3], precv.at[3], partner))
     finish(0)
-    write = pltpu.make_async_copy(fin.at[0], out.at[:, :, mine], lsem.at[16])
+    write = pltpu.make_async_copy(fin.at[0], out.at[:, :, mine], lsem.at[17])
     write.start()
     write.wait()
     arrived(out.at[:, :, theirs], precv.at[3])
@@ -519,14 +532,15 @@
             pltpu.VMEM((TB, 384, 128), BF),
             pltpu.VMEM((192, TB, 128), BF),
             pltpu.VMEM((48, 4 * TB, 128), BF),
-            pltpu.VMEM((2, NCH, 18, TCH, 128), BF),
+            pltpu.VMEM((2, 4, 18, 32, 128), BF),
+            pltpu.VMEM((2, 3, 6, 32, 128), BF),
             pltpu.VMEM((2, 6, 128, 128), BF),
             pltpu.VMEM((3, 12, 128, 128), BF),
-            pltpu.VMEM((3, 12, 128, 128), BF),
+            pltpu.VMEM((2, 12, 128, 128), BF),
             pltpu.VMEM((12, 128, 128), F32),
             pltpu.VMEM((16, TB, 128), BF),
             pltpu.VMEM((16, TB, 384), BF),
-            pltpu.VMEM((TCH, 144, 128), BF),
+            pltpu.VMEM((32, 144, 128), BF),
             pltpu.VMEM((TB, 128), BF),
             pltpu.VMEM((128, 384), BF),
             pltpu.VMEM((128, 384), BF),
@@ -542,15 +556,15 @@
             pltpu.VMEM((256, 128), F32),
             pltpu.VMEM((256, 128), F32),
             pltpu.SMEM((33,), jnp.int32),
-            dma((17,)),
+            dma((18,)),
             dma((4,)),
             dma((4,)),
             dma((48,)),
             dma((48,)),
             dma((17,)),
             dma((17,)),
-            dma((36,)),
-            dma((36,)),
+            dma((42,)),
+            dma((42,)),
             dma((6,)),
             dma((6,)),
         ],

time: 112 us -> 110 us (0.982)
  Pallas kernels: 110 us -> 108 us
    pallas_call x1, Pallas kernels: 110 us -> 108 us  [shards(): pl.pallas_call(body, out_shape=jax.ShapeDtypeStruct((6, 128, 256), BF), i...]
where the time goes in v5:
time: 110 us
  Pallas kernels  108 us (98%)
  local copies, waits for them, and re-layouts  1.77 us (2%)
    pallas_call x1, Pallas kernels, shards(): pl.pallas_call(body, out_shape=jax.ShapeDtypeStruct((6, 128, 256), BF), i...  108 us

profile of v5, /device:TPU:1, one launch (start us, length us, event | category | flops | bytes accessed | tf_op | source)
XLA Modules:
  0.0 109.9 jit_solution(13104624554492640043)
XLA Ops:
  0.0 108.1 %fmm.1 = bf16[6,128,256]{2,1,0:T(8,128)(2,1)} custom-call(bf16[6,128,256]{2,1,0:T(8,128)(2,1)} %bitcast.12, bf16[1536,128]{1,0:T(8,128)(2,1)} %rad_in.1, bf16[128,1536]{1,0:T(8,128)(2,1)} %rcv_in.1, bf16[6,27,128,128]{3,2,1,0:T(8,128)(2,1)} %bitcast.10, s32[6,1,27]{2,1,0:T(1,128)} %bitcast.15, bf16[316,1536]{1,0:T(8,128)(2,1)} %tt_in.1, s32[48,192]{1,0:T(8,128)} %bitcast.13, ...), custom_call_target="tpu_custom_call" | custom-call | tf_op jit(solution)/shard_map/fmm/pallas_call | solution.py:523
  108.1 1.8 %copy.11 = bf16[1,6,128,256]{3,2,1,0:T(8,128)(2,1)} copy(bf16[1,6,128,256]{3,2,1,0:T(8,128)(2,1)} %bitcast.11) | data formatting | bytes 786432

commit v6 on v5

--- a/solution.py
+++ b/solution.py
@@ -168,16 +168,6 @@
         ref[0:128, :] = jnp.transpose(stage[:, 0:128])
         ref[128:256, :] = jnp.transpose(stage[:, 128:256])
 
-    loads["src"].wait()
-    table(slot_of(sraw[0], False).astype(F32), src)
-    loads["tid"].wait()
-    table(sraw[1].astype(F32), tid)
-    loads["tt"].wait()
-    wide[...] = jnp.zeros((384, 384), F32)
-    wide[0:316, :] = tts[...].astype(F32)
-    tt_t[...] = jnp.transpose(wide[...]).astype(BF)
-    loads["rad"].wait()
-
     def pattern_block(at, box):
         for i in range(8):
             two = jnp.concatenate([cur[box(2 * i)], cur[box(2 * i + 1)]], axis=1)
@@ -300,10 +290,19 @@
     got_main(0, 3, 12, RIM, 2)
     send_main(0, 3, HALF, BLK - HALF, b_dn, 0, 2, 1)
     got_main(0, 1, 12, RIM, 2)
+    loads["src"].wait()
+    table(slot_of(sraw[0], False).astype(F32), src)
+    loads["tid"].wait()
+    table(sraw[1].astype(F32), tid)
+    loads["tt"].wait()
+    wide[...] = jnp.zeros((384, 384), F32)
+    wide[0:316, :] = tts[...].astype(F32)
+    tt_t[...] = jnp.transpose(wide[...]).astype(BF)
+    loads["rad"].wait()
+    halves(2, 0)
+    line_event(line2)
     mats(0, 1)
     patterns((0, 0))
-    halves(2, 0)
-    line_event(line2)
     mats(1, 2)
     patterns((1, 0))
     ring_event(line1)

time: 110 us -> 110 us (level)
  no operation moved by 1% of the time
where the time goes in v6:
time: 110 us
  Pallas kernels  108 us (98%)
  local copies, waits for them, and re-layouts  1.77 us (2%)
    pallas_call x1, Pallas kernels, shards(): pl.pallas_call(body, out_shape=jax.ShapeDtypeStruct((6, 128, 256), BF), i...  108 us

profile of v6, /device:TPU:1, one launch (start us, length us, event | category | flops | bytes accessed | tf_op | source)
XLA Modules:
  0.0 109.9 jit_solution(12997690269082420774)
XLA Ops:
  0.0 108.1 %fmm.1 = bf16[6,128,256]{2,1,0:T(8,128)(2,1)} custom-call(bf16[6,128,256]{2,1,0:T(8,128)(2,1)} %bitcast.12, bf16[1536,128]{1,0:T(8,128)(2,1)} %rad_in.1, bf16[128,1536]{1,0:T(8,128)(2,1)} %rcv_in.1, bf16[6,27,128,128]{3,2,1,0:T(8,128)(2,1)} %bitcast.10, s32[6,1,27]{2,1,0:T(1,128)} %bitcast.15, bf16[316,1536]{1,0:T(8,128)(2,1)} %tt_in.1, s32[48,192]{1,0:T(8,128)} %bitcast.13, ...), custom_call_target="tpu_custom_call" | custom-call | tf_op jit(solution)/shard_map/fmm/pallas_call | solution.py:522
  108.1 1.8 %copy.11 = bf16[1,6,128,256]{3,2,1,0:T(8,128)(2,1)} copy(bf16[1,6,128,256]{3,2,1,0:T(8,128)(2,1)} %bitcast.11) | data formatting | bytes 786432
